TPU v7x, 1024 devices: a whole 4x8x16 slice. The times are simulated.
1024 devices in a mesh: member: 16 (over y, x_hi), tile: 64 (over x_lo, z, core).
Axes of the slice: x: 4 (x_hi: 2, x_lo: 2; x = x_hi * 2 + x_lo), y: 8, z: 16, core: 2. Of those that a mesh axis runs over, the one named last changes fastest.
Arguments:
- state: bfloat16 [128, 4, 1024, 128], P('member', None, 'tile'), may hold values from -6 to 6
- first_weight: bfloat16 [32, 4, 3, 3], replicated, may hold values from -1 to 1
- middle_weight: bfloat16 [1, 32, 32, 3, 3], replicated, may hold values from -0.375 to 0.375
- last_weight: bfloat16 [4, 32, 3, 3], replicated, may hold values from -0.375 to 0.375
- observations: float32 [64, 16, 512], P('tile', 'member'), may hold values from -6 to 6
- obs_variance: float32 [64, 16, 512], P('tile', 'member'), may hold values from 0.5 to 4
- observation_rows: int32 [64, 16, 512], P('tile', 'member'), may hold values from 0 to 1535
- loc_class: int32 [64, 16, 512], P('tile', 'member'), may hold values from 0 to 7
Outputs:
- analysis: bfloat16 [128, 4, 1024, 128], P('member', None, 'tile')
Inputs may be any that keep to these rules, and one draw needn't show every extreme that they name: `observation_rows`: each observation of patch (t, j) reads one field at one point of the patches (t - 1, j), (t, j) or (t + 1, j), tiles taken cyclically.
All inputs are finite; a program needn't handle non-finite values.
Results may differ from a plain program's by a relative error of at most 0.0054.
Values may be sent and summed in bfloat16 or wider, within the bound.
No kernel may reach another device: no remote copies, remote signals or barrier semaphores. Data moves between devices by JAX's collectives and lax.ppermute only.
A program may use at most 128 MiB of HBM per device.

v0:
```python
import jax
import jax.numpy as jnp
from jax import lax
from jax.sharding import PartitionSpec as P

NS_ITERS = 4


def with_halo(cells, sides, width):
    for axis, dim in sides:
        count = lax.axis_size(axis)
        head = lax.slice_in_dim(cells, 0, width, axis=dim)
        tail = lax.slice_in_dim(cells, cells.shape[dim] - width, cells.shape[dim], axis=dim)
        cells = jnp.concatenate(
            [
                lax.ppermute(tail, axis, [(i, (i + 1) % count) for i in range(count)]),
                cells,
                lax.ppermute(head, axis, [((i + 1) % count, i) for i in range(count)]),
            ],
            axis=dim,
        )
    return cells


def apply_kernel_lines(padded_rows, weights):
    in_count, members_local, padded_count, width = padded_rows.shape
    out_rows = padded_count - 2
    out_count = weights.shape[0]
    stacked_taps = []
    for row_shift in range(3):
        band = padded_rows[:, :, row_shift : row_shift + out_rows, :]
        for col_shift in range(3):
            stacked_taps.append(jnp.roll(band, 1 - col_shift, axis=3))
    columns = jnp.stack(stacked_taps, axis=0).reshape(
        9 * in_count, members_local * out_rows * width
    )
    flat_weight = jnp.transpose(weights, (0, 2, 3, 1)).reshape(out_count, 9 * in_count)
    summed = jnp.dot(flat_weight, columns, preferred_element_type=jnp.float32)
    return summed.reshape(out_count, members_local, out_rows, width)


def assimilate(obs_ens, background, observed, variance, classes):
    ensemble_size = background.shape[0]
    obs_mean = jnp.mean(obs_ens, axis=1)
    obs_anom = obs_ens - obs_mean[:, None]
    obs_weight = jnp.exp(-0.25 * classes.astype(jnp.float32)) / variance
    identity = jnp.eye(ensemble_size, dtype=jnp.float32)
    highest = lax.Precision.HIGHEST
    gram = (ensemble_size - 1.0) * identity + jnp.dot(
        obs_anom.T,
        obs_weight[:, None] * obs_anom,
        precision=highest,
        preferred_element_type=jnp.float32,
    )
    norm_scale = jnp.sqrt(jnp.sum(gram * gram))
    iterate_y = gram / norm_scale
    iterate_z = identity
    for sweep in range(NS_ITERS):
        middle_factor = 1.5 * identity - 0.5 * jnp.dot(
            iterate_z, iterate_y, precision=highest, preferred_element_type=jnp.float32
        )
        iterate_y = jnp.dot(
            iterate_y, middle_factor, precision=highest, preferred_element_type=jnp.float32
        )
        iterate_z = jnp.dot(
            middle_factor, iterate_z, precision=highest, preferred_element_type=jnp.float32
        )
    root_inv = iterate_z / jnp.sqrt(norm_scale)
    measurement_residual = jnp.dot(
        obs_anom.T,
        obs_weight * (observed - obs_mean),
        precision=highest,
        preferred_element_type=jnp.float32,
    )
    mean_weights = jnp.dot(
        root_inv,
        jnp.dot(
            root_inv, measurement_residual, precision=highest, preferred_element_type=jnp.float32
        ),
        precision=highest,
        preferred_element_type=jnp.float32,
    )
    transform = jnp.sqrt(ensemble_size - 1.0) * root_inv + mean_weights[:, None]
    back = background.astype(jnp.float32)
    back_mean = jnp.mean(back, axis=0)
    back_anom = back - back_mean[None, :]
    result = back_mean[None, :] + jnp.dot(
        transform.T, back_anom, precision=highest, preferred_element_type=jnp.float32
    )
    return result.astype(jnp.bfloat16)


def analyse(neighbours, observed, variance, rows_read, classes):
    span = neighbours.shape[2]
    source_part = rows_read // span
    offset = rows_read % span
    obs_ens = neighbours[source_part, :, offset].astype(jnp.float32)
    return assimilate(obs_ens, neighbours[1], observed, variance, classes)


def local(
    state,
    first_weight,
    middle_weight,
    last_weight,
    observations,
    obs_variance,
    observation_rows,
    loc_class,
):
    patch_members, field_stack, tile_rows, width = state.shape
    depth_total = middle_weight.shape[0] + 2
    weight_list = [first_weight] + [middle_weight[0]] + [last_weight]
    feature_major_layout = jnp.transpose(state, (1, 0, 2, 3))
    hidden = with_halo(feature_major_layout, (("tile", 2),), depth_total)
    for number in range(depth_total):
        element_count = apply_kernel_lines(hidden, weight_list[number])
        if number + 1 < depth_total:
            hidden = jax.nn.silu(element_count).astype(jnp.bfloat16)
    prediction_major_layout = (feature_major_layout.astype(jnp.float32) + element_count).astype(
        jnp.bfloat16
    )
    step_member_states = jnp.transpose(prediction_major_layout, (1, 0, 2, 3))
    row_bands = lax.axis_size("member")
    points_per_patch = tile_rows // row_bands * width
    ensemble = lax.all_to_all(step_member_states, "member", split_axis=2, concat_axis=0, tiled=True)
    ensemble_size = ensemble.shape[0]
    owned = ensemble.reshape(1, ensemble_size, field_stack * points_per_patch)
    neighbours = with_halo(owned, (("tile", 0),), 1)
    analysed = analyse(
        neighbours, observations[0, 0], obs_variance[0, 0], observation_rows[0, 0], loc_class[0, 0]
    )
    outbound_values = analysed.reshape(ensemble_size, field_stack, 1, points_per_patch)
    returned = lax.all_to_all(outbound_values, "member", split_axis=0, concat_axis=2, tiled=True)
    return returned


def solution(mesh):
    return jax.shard_map(
        local,
        mesh=mesh,
        in_specs=(
            P("member", None, "tile", None),
            P(),
            P(),
            P(),
            P("tile", "member", None),
            P("tile", "member", None),
            P("tile", "member", None),
            P("tile", "member", None),
        ),
        out_specs=P("member", None, "tile", None),
        check_vma=False,
    )
```

profile of v0, /device:TPU:2, one launch (start us, length us, event | category | flops | bytes accessed | tf_op | source)
XLA Modules:
  0.0 174.3 jit_solution(3656001303512898576)
XLA Ops:
  1.0 1.9 %collective-permute-start = (bf16[4,8,3,128]{3,1,0,2:T(8,128)(2,1)S(1)}, bf16[4,8,3,128]{3,1,0,2:T(8,128)(2,1)S(1)}, u32[]{:S(2)}, u32[]{:S(2)}) collective-permute-start(bf16[4,8,3,128]{3,1,0,2:T(8,128)(2,1)S(1)} %get-tuple-element.41), channel_id=1, source_target_pairs={{0,1},{1,2},{2,3},{3,4},{4,5},{5,6},{6,7},{7,8},{8,9},{9,10},{10,1... | collective-permute-start | bytes 73736 | tf_op jit(solution)/shard_map/ppermute | solution.py:16
  2.9 17.6 %collective-permute-start.1 = (bf16[4,8,3,128]{3,1,0,2:T(8,128)(2,1)S(1)}, bf16[4,8,3,128]{3,1,0,2:T(8,128)(2,1)S(1)}, u32[]{:S(2)}, u32[]{:S(2)}) collective-permute-start(bf16[4,8,3,128]{3,1,0,2:T(8,128)(2,1)S(1)} %get-tuple-element.42), channel_id=1, source_target_pairs={{1,0},{2,1},{3,2},{4,3},{5,4},{6,5},{7,6},{8,7},{9,8},{10,9},{11,1... | collective-permute-start | bytes 73736 | tf_op jit(solution)/shard_map/ppermute | solution.py:18
  26.2 2.1 %convolution_bitcast_fusion = f32[32,20480]{1,0:T(8,128)} fusion(bf16[36,20480]{1,0:T(8,128)(2,1)S(1)} %reshape.189, bf16[32,36]{0,1:T(8,128)(2,1)S(1)} %reshape.190), kind=kOutput, calls=%fused_computation.1 | convolution fusion | flops 47185920 | bytes 4098304 | tf_op jit(solution)/shard_map/dot_general | solution.py:38
  28.3 2.0 %reshape.191 = f32[32,8,20,128]{3,2,1,0:T(8,128)S(1)} reshape(f32[32,20480]{1,0:T(8,128)} %convolution_bitcast_fusion) | data formatting | bytes 5242880 | tf_op jit(solution)/shard_map/reshape | solution.py:39
  31.1 2.8 %fusion.58 = (bf16[32,8,18,127]{3,2,1,0:T(8,128)(2,1)S(1)}, bf16[32,8,18,127]{3,2,1,0:T(8,128)(2,1)S(1)}, bf16[32,8,18,127]{3,2,1,0:T(8,128)(2,1)S(1)}, bf16[32,...) fusion(bf16[32,8,20,128]{3,2,1,0:T(8,128)(2,1)S(1)} %multiply_convert_fu, ...), kind=kLoop, calls=%fused_computation.123 | loop fusion | bytes 14045184 | tf_op jit(solution)/shard_map/jit(_roll_static)/slice | solution.py:33
  34.0 2.8 %fusion.59 = (bf16[32,8,18,1]{3,2,1,0:T(8,128)(2,1)S(1)}, bf16[32,8,18,1]{3,2,1,0:T(8,128)(2,1)S(1)}, bf16[32,8,18,1]{3,2,1,0:T(8,128)(2,1)S(1)}, bf16[32,8,18,1...) fusion(bf16[32,8,20,128]{3,2,1,0:T(8,128)(2,1)S(1)} %multiply_convert_fusion.1), kind=kLoop, calls=%fused_computation.124 | loop fusion | bytes 110592 | tf_op jit(solution)/shard_map/jit(_roll_static)/slice | solution.py:33
  36.8 2.1 %fusion.3 = bf16[9,32,8,18,128]{4,3,2,1,0:T(8,128)(2,1)} fusion(bf16[32,8,18,127]{3,2,1,0:T(8,128)(2,1)S(1)} %get-tuple-element.22, bf16[32,8,18,1]{3,2,1,0:T(8,128)(2,1)S(1)} %get-tuple-element.28), kind=kLoop, calls=%fused_computation.12 | loop fusion | flops 2359295 | bytes 2752512
  40.3 2.1 %fusion.4 = bf16[9,32,8,18,128]{4,3,2,1,0:T(8,128)(2,1)} fusion(bf16[9,32,8,18,128]{4,3,2,1,0:T(8,128)(2,1)} %fusion.2, bf16[32,8,18,1]{3,2,1,0:T(8,128)(2,1)S(1)} %get-tuple-element.27, bf16[32,8,18,127]{3,2,1,0:T(8,128)(2,1)S(1)} %get-tuple-element.21), kind=kLoop, calls=%fused_computation.14 | loop fusion | flops 2359296 | bytes 2752512
  42.4 2.1 %fusion.5 = bf16[9,32,8,18,128]{4,3,2,1,0:T(8,128)(2,1)} fusion(bf16[9,32,8,18,128]{4,3,2,1,0:T(8,128)(2,1)} %fusion.4, bf16[32,8,18,127]{3,2,1,0:T(8,128)(2,1)S(1)} %get-tuple-element.20, bf16[32,8,18,1]{3,2,1,0:T(8,128)(2,1)S(1)} %get-tuple-element.26), kind=kLoop, calls=%fused_computation.16 | loop fusion | flops 2359296 | bytes 2752512
  44.5 2.0 %fusion.1 = bf16[9,32,8,18,128]{4,3,2,1,0:T(8,128)(2,1)} fusion(bf16[9,32,8,18,128]{4,3,2,1,0:T(8,128)(2,1)} %fusion.5, bf16[32,8,20,128]{3,2,1,0:T(8,128)(2,1)S(1)} %multiply_convert_fusion.1), kind=kLoop, calls=%fused_computation.8 | loop fusion | bytes 2752512
  46.6 2.2 %fusion.6 = bf16[9,32,8,18,128]{4,3,2,1,0:T(8,128)(2,1)} fusion(bf16[9,32,8,18,128]{4,3,2,1,0:T(8,128)(2,1)} %fusion.1, bf16[32,8,18,1]{3,2,1,0:T(8,128)(2,1)S(1)} %get-tuple-element.25, bf16[32,8,18,127]{3,2,1,0:T(8,128)(2,1)S(1)} %get-tuple-element.19), kind=kLoop, calls=%fused_computation.18 | loop fusion | flops 2359296 | bytes 2752512
  48.8 2.1 %fusion.7 = bf16[9,32,8,18,128]{4,3,2,1,0:T(8,128)(2,1)} fusion(bf16[9,32,8,18,128]{4,3,2,1,0:T(8,128)(2,1)} %fusion.6, bf16[32,8,18,127]{3,2,1,0:T(8,128)(2,1)S(1)} %get-tuple-element.18, bf16[32,8,18,1]{3,2,1,0:T(8,128)(2,1)S(1)} %get-tuple-element.24), kind=kLoop, calls=%fused_computation.20 | loop fusion | flops 2359296 | bytes 2752512
  50.9 2.1 %fusion = bf16[9,32,8,18,128]{4,3,2,1,0:T(8,128)(2,1)} fusion(bf16[9,32,8,18,128]{4,3,2,1,0:T(8,128)(2,1)} %fusion.7, bf16[32,8,20,128]{3,2,1,0:T(8,128)(2,1)S(1)} %multiply_convert_fusion.1), kind=kLoop, calls=%fused_computation.6 | loop fusion | bytes 2752512
  52.9 2.1 %fusion.8 = bf16[9,32,8,18,128]{4,3,2,1,0:T(8,128)(2,1)} fusion(bf16[9,32,8,18,128]{4,3,2,1,0:T(8,128)(2,1)} %fusion, bf16[32,8,18,1]{3,2,1,0:T(8,128)(2,1)S(1)} %get-tuple-element.23, bf16[32,8,18,127]{3,2,1,0:T(8,128)(2,1)S(1)} %get-tuple-element.17), kind=kLoop, calls=%fused_computation.22 | loop fusion | flops 2359296 | bytes 2752512 | tf_op jit(solution)/shard_map/stack | solution.py:34
  55.0 16.8 %reshape.192 = bf16[288,18432]{1,0:T(8,128)(2,1)} reshape(bf16[9,32,8,18,128]{4,3,2,1,0:T(8,128)(2,1)} %fusion.8) | data formatting | bytes 21233664 | tf_op jit(solution)/shard_map/reshape | solution.py:34
  71.8 7.5 %convolution_bitcast_fusion.1 = f32[32,18432]{1,0:T(8,128)} fusion(bf16[32,288]{1,0:T(8,128)(2,1)S(1)} %reshape.193, bf16[288,18432]{1,0:T(8,128)(2,1)} %reshape.192), kind=kOutput, calls=%fused_computation.2 | convolution fusion | flops 339738624 | bytes 12994560 | tf_op jit(solution)/shard_map/dot_general | solution.py:38
  99.3 14.8 %reshape.195 = bf16[288,16384]{1,0:T(8,128)(2,1)} reshape(bf16[9,32,8,16,128]{4,3,2,1,0:T(8,128)(2,1)} %fusion.22) | data formatting | bytes 18874368 | tf_op jit(solution)/shard_map/reshape | solution.py:34
  114.1 5.0 %convolution_bitcast_fusion.2 = f32[1,4,128,128]{3,1,2,0:T(4,128)S(1)} fusion(bf16[288,16384]{1,0:T(8,128)(2,1)} %reshape.195, bf16[4,288]{1,0:T(4,128)(2,1)S(1)} %reshape.196), kind=kOutput, calls=%fused_computation.24 | convolution fusion | flops 37748736 | bytes 9701632 | tf_op jit(solution)/shard_map/dot_general | solution.py:38
  120.0 9.1 %all-to-all-start = ((bf16[8,4,16,128]{3,0,1,2:T(8,128)(2,1)}), bf16[8,4,16,128]{3,0,1,2:T(8,128)(2,1)S(1)}, u32[]{:S(2)}, u32[]{:S(2)}) async-start(bf16[8,4,16,128]{3,0,1,2:T(8,128)(2,1)} %fusion.38), calls=%async_computation | async-start | bytes 262144 | tf_op jit(solution)/shard_map/all_to_all | solution.py:126
  129.1 11.0 %all-to-all-done = bf16[8,4,16,128]{3,0,1,2:T(8,128)(2,1)S(1)} async-done(((bf16[8,4,16,128]{3,0,1,2:T(8,128)(2,1)}), bf16[8,4,16,128]{3,0,1,2:T(8,128)(2,1)S(1)}, u32[]{:S(2)}, u32[]{:S(2)}) %all-to-all-start) | async-done | bytes 131104 | tf_op jit(solution)/shard_map/all_to_all | solution.py:126
  140.3 1.9 %collective-permute-start.2 = (bf16[1,128,512]{1,2,0:T(8,128)(2,1)S(1)}, bf16[1,128,512]{1,2,0:T(8,128)(2,1)S(1)}, u32[]{:S(2)}, u32[]{:S(2)}) collective-permute-start(bf16[1,128,512]{1,2,0:T(8,128)(2,1)S(1)} %copy.27), channel_id=1, source_target_pairs={{0,1},{1,2},{2,3},{3,4},{4,5},{5,6},{6,7},{7,8},{8,9},{9,10},{10,1... | collective-permute-start | bytes 393224 | tf_op jit(solution)/shard_map/ppermute | solution.py:16
  142.2 5.8 %collective-permute-start.3 = (bf16[1,128,512]{1,2,0:T(8,128)(2,1)S(1)}, bf16[1,128,512]{1,2,0:T(8,128)(2,1)S(1)}, u32[]{:S(2)}, u32[]{:S(2)}) collective-permute-start(bf16[1,128,512]{1,2,0:T(8,128)(2,1)S(1)} %copy.27), channel_id=1, source_target_pairs={{1,0},{2,1},{3,2},{4,3},{5,4},{6,5},{7,6},{8,7},{9,8},{10,9},{11,1... | collective-permute-start | bytes 393224 | tf_op jit(solution)/shard_map/ppermute | solution.py:18
  150.5 3.2 %gather_fusion = bf16[512,128]{1,0:T(8,128)(2,1)S(1)} fusion(bf16[3,128,512]{1,2,0:T(8,128)(2,1)S(1)} %pad_maximum_fusion, s32[512]{0:T(512)S(1)} %bitcast.215), kind=kCustom, calls=%fused_computation | custom fusion | bytes 266240 | tf_op jit(solution)/shard_map/gather | solution.py:97
  159.7 13.9 %all_to_all.33 = bf16[128,4,1,128]{3,1,2,0:T(4,128)(2,1)S(1)} all-to-all(bf16[128,4,1,128]{3,1,2,0:T(4,128)(2,1)S(1)} %bitcast.220), channel_id=1, replica_groups=mesh['member'=16,'tile'=64] {'member'}, dimensions={0} | all-to-all | bytes 262144 | tf_op jit(solution)/shard_map/all_to_all | solution.py:134
  (79 shorter events, 38.1 us)
Async XLA Ops:
  1.0 22.1 %collective-permute-start = (bf16[4,8,3,128]{3,1,0,2:T(8,128)(2,1)S(1)}, bf16[4,8,3,128]{3,1,0,2:T(8,128)(2,1)S(1)}, u32[]{:S(2)}, u32[]{:S(2)}) collective-permute-start(bf16[4,8,3,128]{3,1,0,2:T(8,128)(2,1)S(1)} %get-tuple-element.41), channel_id=1, source_target_pairs={{0,1},{1,2},{2,3},{3,4},{4,5},{5,6},{6,7},{7,8},{8,9},{9,10},{10,1... | collective-permute-start | bytes 73736 | tf_op jit(solution)/shard_map/ppermute | solution.py:16
  2.9 20.2 %collective-permute-start.1 = (bf16[4,8,3,128]{3,1,0,2:T(8,128)(2,1)S(1)}, bf16[4,8,3,128]{3,1,0,2:T(8,128)(2,1)S(1)}, u32[]{:S(2)}, u32[]{:S(2)}) collective-permute-start(bf16[4,8,3,128]{3,1,0,2:T(8,128)(2,1)S(1)} %get-tuple-element.42), channel_id=1, source_target_pairs={{1,0},{2,1},{3,2},{4,3},{5,4},{6,5},{7,6},{8,7},{9,8},{10,9},{11,1... | collective-permute-start | bytes 73736 | tf_op jit(solution)/shard_map/ppermute | solution.py:18
  114.1 5.1 %copy-start = (bf16[8,4,16,128]{3,2,1,0:T(8,128)(2,1)S(1)}, bf16[8,4,16,128]{3,2,1,0:T(8,128)(2,1)}, u32[]{:S(2)}) copy-start(bf16[8,4,16,128]{3,2,1,0:T(8,128)(2,1)} %param.8) | copy-start | bytes 393220
  114.1 15.0 %copy-start.4 = (s32[1,1,512]{2,1,0:T(1,128)S(1)}, s32[1,1,512]{2,1,0:T(1,128)}, u32[]{:S(2)}) copy-start(s32[1,1,512]{2,1,0:T(1,128)} %param.14) | copy-start | bytes 6148
  114.1 15.0 %copy-start.1 = (f32[1,1,512]{2,1,0:T(1,128)S(1)}, f32[1,1,512]{2,1,0:T(1,128)}, u32[]{:S(2)}) copy-start(f32[1,1,512]{2,1,0:T(1,128)} %param.13) | copy-start | bytes 6148
  114.1 15.1 %copy-start.2 = (s32[1,1,512]{2,1,0:T(1,128)S(1)}, s32[1,1,512]{2,1,0:T(1,128)}, u32[]{:S(2)}) copy-start(s32[1,1,512]{2,1,0:T(1,128)} %param.15) | copy-start | bytes 6148
  119.1 34.7 %copy-start.3 = (f32[1,1,512]{2,1,0:T(1,128)S(1)}, f32[1,1,512]{2,1,0:T(1,128)}, u32[]{:S(2)}) copy-start(f32[1,1,512]{2,1,0:T(1,128)} %param.12) | copy-start | bytes 6148
  120.0 20.2 %all-to-all-start = ((bf16[8,4,16,128]{3,0,1,2:T(8,128)(2,1)}), bf16[8,4,16,128]{3,0,1,2:T(8,128)(2,1)S(1)}, u32[]{:S(2)}, u32[]{:S(2)}) async-start(bf16[8,4,16,128]{3,0,1,2:T(8,128)(2,1)} %fusion.38), calls=%async_computation | async-start | bytes 262144 | tf_op jit(solution)/shard_map/all_to_all | solution.py:126
  140.3 8.4 %collective-permute-start.2 = (bf16[1,128,512]{1,2,0:T(8,128)(2,1)S(1)}, bf16[1,128,512]{1,2,0:T(8,128)(2,1)S(1)}, u32[]{:S(2)}, u32[]{:S(2)}) collective-permute-start(bf16[1,128,512]{1,2,0:T(8,128)(2,1)S(1)} %copy.27), channel_id=1, source_target_pairs={{0,1},{1,2},{2,3},{3,4},{4,5},{5,6},{6,7},{7,8},{8,9},{9,10},{10,1... | collective-permute-start | bytes 393224 | tf_op jit(solution)/shard_map/ppermute | solution.py:16
  142.2 8.3 %collective-permute-start.3 = (bf16[1,128,512]{1,2,0:T(8,128)(2,1)S(1)}, bf16[1,128,512]{1,2,0:T(8,128)(2,1)S(1)}, u32[]{:S(2)}, u32[]{:S(2)}) collective-permute-start(bf16[1,128,512]{1,2,0:T(8,128)(2,1)S(1)} %copy.27), channel_id=1, source_target_pairs={{1,0},{2,1},{3,2},{4,3},{5,4},{6,5},{7,6},{8,7},{9,8},{10,9},{11,1... | collective-permute-start | bytes 393224 | tf_op jit(solution)/shard_map/ppermute | solution.py:18
where the time goes:
time: 176 us; the launch traced here: 174 us
  local copies, waits for them, and re-layouts  64.1 us (36%)
  starting transfers between devices  36.3 us (21%)
  other arithmetic  25.8 us (15%)
  matrix products  19.6 us (11%)
  blocking collectives  13.9 us (8%)
  waiting for transfers between devices  13.5 us (8%)
    reshape x3, local copies, waits for them, and re-layouts, apply_kernel_lines(): jnp.stack(stacked_taps, axis=0)  32.5 us
    ppermute x2, starting transfers between devices, with_halo(): lax.ppermute(head, axis, [((i + 1) % count, i) for i in range(count)])  23.4 us
    unnamed x15, other arithmetic  19.2 us
    dot_general x3, matrix products, apply_kernel_lines(): summed = jnp.dot(flat_weight, columns, preferred_element_type=jnp.float32)  14.6 us
    all_to_all x1, blocking collectives, local(): lax.all_to_all(outbound_values, 'member', split_axis=0, concat_axis=2, ti...  13.9 us
    all_to_all x1, waiting for transfers between devices, local(): lax.all_to_all(step_member_states, 'member', split_axis=2, concat_axis=0,...  11 us
    unnamed x21, local copies, waits for them, and re-layouts  10.8 us
    slice x6, local copies, waits for them, and re-layouts, apply_kernel_lines(): stacked_taps.append(jnp.roll(band, 1 - col_shift, axis=3))  9.72 us
  transfers between devices with their start and end apart: 5, of which 3 were waited for; matrix products, arithmetic and copies ran while one was open for 2% of the time, Pallas kernels for 0%

commit v1 on v0

v1 whole, which is shorter than its diff:
```python
import jax
import jax.numpy as jnp
from jax import lax
from jax.experimental import pallas as pl
from jax.experimental.pallas import tpu as pltpu
from jax.sharding import PartitionSpec as P

NS_ITERS = 4
F32 = jnp.float32
BF16 = jnp.bfloat16
VMEM = pl.BlockSpec(memory_space=pltpu.VMEM)


def params(mib):
    return pltpu.CompilerParams(vmem_limit_bytes=mib << 20)


def silu(v):
    half = 0.5 * v
    return half + half * jnp.tanh(half)


def iota(shape, axis):
    return lax.broadcasted_iota(jnp.int32, shape, axis)


def pick(distance, choices):
    out = jnp.zeros(distance.shape, F32)
    for tap, value in enumerate(choices):
        out = jnp.where(distance == tap, value, out)
    return out


def edges_kernel(state_ref, head_ref, tail_ref, wide):
    wide[...] = state_ref[...].astype(F32)
    for row in range(3):
        head_ref[row * 32 : (row + 1) * 32, :] = wide[pl.ds(row, 32, stride=16), :].astype(BF16)
        tail_ref[row * 32 : (row + 1) * 32, :] = wide[pl.ds(13 + row, 32, stride=16), :].astype(BF16)


def weights_kernel(first_ref, middle_ref, last_ref, t1_ref, t2_ref, t3_ref):
    where_to = iota((4, 192), 1) // 16
    expanded = []
    for dy in range(3):
        total = jnp.zeros((32, 192), F32)
        for dx in range(3):
            spread = (where_to == iota((4, 192), 0) + 4 * dx).astype(BF16)
            total += lax.dot_general(
                first_ref[dy * 3 + dx], spread, (((0,), (0,)), ((), ())), preferred_element_type=F32
            )
        expanded.append(jnp.concatenate([total] * 10, axis=0))
    distance = iota((320, 192), 1) % 16 - iota((320, 192), 0) // 32
    t1_ref[...] = pick(distance, expanded).astype(BF16)
    distance = iota((192, 256), 1) // 32 - iota((192, 256), 0) // 32
    for dx in range(3):
        taps = []
        for dy in range(3):
            one = middle_ref[dy * 3 + dx].astype(F32)
            wide = jnp.concatenate([one] * 8, axis=1)
            taps.append(jnp.concatenate([wide] * 6, axis=0))
        t2_ref[dx * 192 : (dx + 1) * 192, :] = pick(distance, taps).astype(BF16)
    distance = iota((64, 640), 1) // 32 - iota((64, 640), 0) % 16
    for dx in range(3):
        taps = []
        for dy in range(3):
            one = last_ref[dy * 3 + dx].astype(F32)
            wide = jnp.concatenate([one] * 4, axis=1)
            rows = jnp.concatenate(
                [jnp.broadcast_to(wide[f : f + 1], (16, 128)) for f in range(4)], axis=0
            )
            taps.append(jnp.concatenate([rows] * 5, axis=1))
        t3_ref[dx * 64 : (dx + 1) * 64, :] = pick(distance, taps).astype(BF16)[:, :576]


def forecast_kernel(
    state_ref, above_ref, below_ref, t1_ref, t2_ref, t3_ref, out_ref, wide, padded, h1, h2, sent
):
    wide[...] = state_ref[...].astype(F32)
    nothing = jnp.zeros((32, 128), F32)
    for row in range(16):
        at = pl.ds(row, 32, stride=16)
        if row < 3:
            padded[at, :] = above_ref[row * 32 : (row + 1) * 32, :].astype(F32)
        elif row < 12:
            padded[at, :] = wide[pl.ds(row - 3, 32, stride=16), :]
        else:
            padded[at, :] = nothing
        at = pl.ds(512 + row, 32, stride=16)
        if row < 9:
            padded[at, :] = wide[pl.ds(row + 7, 32, stride=16), :]
        elif row < 12:
            padded[at, :] = below_ref[(row - 9) * 32 : (row - 8) * 32, :].astype(F32)
        else:
            padded[at, :] = nothing
    for pair in range(4):
        members = (2 * pair, 2 * pair + 1)
        slot = pair % 2
        for half in range(2):
            sides = []
            for member in members:
                start = half * 512 + member * 64
                rows = padded[start : start + 64, :]
                sides.append(
                    jnp.concatenate(
                        [pltpu.roll(rows, 1, 1), rows, pltpu.roll(rows, 127, 1)], axis=0
                    ).astype(BF16)
                )
            summed = jnp.dot(
                t1_ref[...], jnp.concatenate(sides, axis=1), preferred_element_type=F32
            )
            h1[slot, half * 320 : (half + 1) * 320, :] = silu(summed).astype(BF16)
        for group in range(3):
            taps = jnp.dot(
                t2_ref[...], h1[slot, group * 192 : group * 192 + 256, :], preferred_element_type=F32
            )
            for side in range(2):
                part = taps[:, side * 128 : (side + 1) * 128]
                summed = (
                    part[192:384]
                    + pltpu.roll(part[:192], 1, 1)
                    + pltpu.roll(part[384:], 127, 1)
                )
                h2[slot, group * 192 : (group + 1) * 192, side * 128 : (side + 1) * 128] = silu(
                    summed
                ).astype(BF16)
        taps = jnp.dot(t3_ref[...], h2[slot], preferred_element_type=F32)
        for side, member in enumerate(members):
            part = taps[:, side * 128 : (side + 1) * 128]
            change = (
                part[64:128] + pltpu.roll(part[:64], 1, 1) + pltpu.roll(part[128:], 127, 1)
            )
            result = wide[member * 64 : (member + 1) * 64, :] + change
            for f in range(4):
                sent[pl.ds(f * 8 + member, 16, stride=32), :] = result[f * 16 : (f + 1) * 16]
    out_ref[...] = sent[...].astype(BF16)


def exact_dot(a, b, contract=((1,), (0,))):
    return lax.dot_general(
        a, b, (contract, ((), ())), precision=lax.Precision.HIGHEST, preferred_element_type=F32
    )


def members_by_points(ref):
    blocks = ref[...].astype(F32).reshape(16, 4, 8, 128)
    return [blocks[:, f].reshape(128, 128) for f in range(4)]


def analysis_kernel(
    above_ref, own_ref, below_ref, obs_ref, var_ref, rows_ref, class_ref, out_ref, held
):
    size = 128
    picked = rows_ref[...]
    entry = iota((256, 512), 0)
    obs_ens = jnp.zeros((size, 512), F32)
    for source, ref in enumerate((above_ref, own_ref, below_ref)):
        blocks = members_by_points(ref)
        if source == 1:
            back = jnp.concatenate(blocks, axis=1)
        for two in range(2):
            values = jnp.concatenate(blocks[2 * two : 2 * two + 2], axis=1).astype(BF16)
            chosen = (entry == picked - (source * 512 + two * 256)).astype(F32).astype(BF16)
            obs_ens += jnp.dot(values, chosen, preferred_element_type=F32)
    obs_mean = jnp.sum(obs_ens, axis=0, keepdims=True) * (1.0 / size)
    anom = obs_ens - obs_mean
    weight = jnp.exp(-0.25 * class_ref[...].astype(F32)) / var_ref[...]
    identity = (iota((size, size), 0) == iota((size, size), 1)).astype(F32)
    gram = (size - 1.0) * identity + exact_dot(anom, anom * weight, ((1,), (1,)))
    residual = jnp.sum(anom * (weight * (obs_ref[...] - obs_mean)), axis=1, keepdims=True)
    square = jnp.sum(jnp.sum(gram * gram, axis=1, keepdims=True), axis=0, keepdims=True)
    norm = jnp.sqrt(square)
    y = gram / norm
    z = 1.5 * identity - 0.5 * y
    y = exact_dot(y, z)
    for sweep in range(1, NS_ITERS):
        factor = 1.5 * identity - 0.5 * exact_dot(z, y)
        if sweep + 1 < NS_ITERS:
            y = exact_dot(y, factor)
        z = exact_dot(factor, z)
    root = z / jnp.sqrt(norm)
    once = jnp.sum(root * residual, axis=0, keepdims=True)
    mean_weights = jnp.sum(root * once, axis=1, keepdims=True)
    back_mean = jnp.sum(back, axis=0, keepdims=True) * (1.0 / size)
    back_anom = back - back_mean
    shift = back_mean + jnp.sum(mean_weights * back_anom, axis=0, keepdims=True)
    result = shift + exact_dot(root * (size - 1.0) ** 0.5, back_anom)
    for f in range(4):
        held[:, f] = result[:, f * 128 : (f + 1) * 128].reshape(16, 8, 128)
    out_ref[...] = held[...].reshape(512, 128).astype(BF16)


def unpack_kernel(in_ref, out_ref, wide):
    wide[...] = in_ref[...].astype(F32)
    for lane in range(32):
        member, f = lane // 4, lane % 4
        out_ref[lane * 16 : (lane + 1) * 16, :] = wide[
            pl.ds(f * 8 + member, 16, stride=32), :
        ].astype(BF16)


def shape(rows, columns=128):
    return jax.ShapeDtypeStruct((rows, columns), BF16)


def scratch(*dims, dtype=F32):
    return pltpu.VMEM(dims, dtype)


def local(
    state,
    first_weight,
    middle_weight,
    last_weight,
    observations,
    obs_variance,
    observation_rows,
    loc_class,
):
    rows = state.reshape(512, 128)
    head, tail = pl.pallas_call(
        edges_kernel,
        out_shape=(shape(96), shape(96)),
        in_specs=[VMEM],
        out_specs=(VMEM, VMEM),
        scratch_shapes=[scratch(512, 128)],
        compiler_params=params(8),
        name="edges",
    )(rows)
    count = lax.axis_size("tile")
    up = [(i, (i + 1) % count) for i in range(count)]
    down = [((i + 1) % count, i) for i in range(count)]
    above = lax.ppermute(tail, "tile", up)
    below = lax.ppermute(head, "tile", down)
    t1, t2, t3 = pl.pallas_call(
        weights_kernel,
        out_shape=(shape(320, 192), shape(576, 256), shape(192, 576)),
        in_specs=[VMEM] * 3,
        out_specs=(VMEM,) * 3,
        compiler_params=params(8),
        cost_estimate=pl.CostEstimate(flops=4000000, bytes_accessed=700000, transcendentals=0),
        name="weights",
    )(
        jnp.transpose(first_weight, (2, 3, 1, 0)).reshape(9, 4, 32),
        jnp.transpose(middle_weight[0], (2, 3, 0, 1)).reshape(9, 32, 32),
        jnp.transpose(last_weight, (2, 3, 0, 1)).reshape(9, 4, 32),
    )
    forecast = pl.pallas_call(
        forecast_kernel,
        out_shape=shape(512),
        in_specs=[VMEM] * 6,
        out_specs=VMEM,
        scratch_shapes=[
            scratch(512, 128),
            scratch(1024, 128),
            scratch(2, 640, 256, dtype=BF16),
            scratch(2, 576, 256, dtype=BF16),
            scratch(512, 128),
        ],
        compiler_params=params(16),
        name="forecast",
    )(rows, above, below, t1, t2, t3)
    own = lax.all_to_all(
        forecast.reshape(16, 32, 128), "member", split_axis=0, concat_axis=0, tiled=True
    ).reshape(512, 128)
    before = lax.ppermute(own, "tile", up)
    after = lax.ppermute(own, "tile", down)
    analysed = pl.pallas_call(
        analysis_kernel,
        out_shape=shape(512),
        in_specs=[VMEM] * 7,
        out_specs=VMEM,
        scratch_shapes=[scratch(16, 4, 8, 128)],
        compiler_params=params(16),
        name="analysis",
    )(
        before,
        own,
        after,
        observations.reshape(1, 512),
        obs_variance.reshape(1, 512),
        observation_rows.reshape(1, 512),
        loc_class.reshape(1, 512),
    )
    returned = lax.all_to_all(
        analysed.reshape(16, 32, 128), "member", split_axis=0, concat_axis=0, tiled=True
    ).reshape(512, 128)
    out = pl.pallas_call(
        unpack_kernel,
        out_shape=shape(512),
        in_specs=[VMEM],
        out_specs=VMEM,
        scratch_shapes=[scratch(512, 128)],
        compiler_params=params(8),
        name="unpack",
    )(returned)
    return out.reshape(8, 4, 16, 128)


def solution(mesh):
    return jax.shard_map(
        local,
        mesh=mesh,
        in_specs=(
            P("member", None, "tile", None),
            P(),
            P(),
            P(),
            P("tile", "member", None),
            P("tile", "member", None),
            P("tile", "member", None),
            P("tile", "member", None),
        ),
        out_specs=P("member", None, "tile", None),
        check_vma=False,
    )
```

time: 176 us -> 79.2 us (0.45)
  local copies, waits for them, and re-layouts: 64.1 us -> 3.19 us
  other arithmetic: 25.8 us -> 0 us
  blocking collectives: 13.9 us -> 33.8 us
  matrix products: 19.6 us -> 0 us
  starting transfers between devices: 36.3 us -> 27.4 us
  Pallas kernels: 0 us -> 7.73 us
  waiting for transfers between devices: 13.5 us -> 6.47 us
    reshape x10 -> x0, local copies, waits for them, and re-layouts: 37.4 us -> none  [the longest x3 32.5 us: apply_kernel_lines(): jnp.stack(stacked_taps, axis=0)]
    all_to_all x1 -> x2, blocking collectives: 13.9 us -> 33.8 us  [the longest x1 20 us: local(): lax.all_to_all(forecast.reshape(16, 32, 128), 'member', split_axis=0, con...]
    dot_general x19 -> x0, matrix products: 19.6 us -> none  [the longest x3 14.6 us: apply_kernel_lines(): summed = jnp.dot(flat_weight, columns, preferred_element_type=jnp.float32)]
    unnamed x15 -> x0, other arithmetic: 19.2 us -> none
    all_to_all x1 -> x0, waiting for transfers between devices: 11 us -> none  [local(): lax.all_to_all(step_member_states, 'member', split_axis=2, concat_axis=0,...]
    slice x7 -> x0, local copies, waits for them, and re-layouts: 9.72 us -> none  [the longest x6 9.72 us: apply_kernel_lines(): stacked_taps.append(jnp.roll(band, 1 - col_shift, axis=3))]
    all_to_all x1 -> x0, starting transfers between devices: 9.06 us -> none  [local(): lax.all_to_all(step_member_states, 'member', split_axis=2, concat_axis=0,...]
    pallas_call x0 -> x5, Pallas kernels: none -> 7.73 us  [the longest x1 3.67 us: local(): pl.pallas_call(forecast_kernel, out_shape=shape(512), in_specs=[VMEM] * 6...]
  transfers between devices with their start and end apart: 5 -> 4, of which waited for: 3 -> 2; matrix products, arithmetic and copies ran while one was open for 2% -> 0% of each run, Pallas kernels for 0% -> 1%
where the time goes in v1:
time: 79.2 us; the launch traced here: 78.8 us
  blocking collectives  33.8 us (43%)
  starting transfers between devices  27.4 us (35%)
  Pallas kernels  7.73 us (10%)
  waiting for transfers between devices  6.47 us (8%)
  local copies, waits for them, and re-layouts  3.19 us (4%)
    all_to_all x1, blocking collectives, local(): lax.all_to_all(forecast.reshape(16, 32, 128), 'member', split_axis=0, con...  20 us
    ppermute x1, starting transfers between devices, local(): below = lax.ppermute(head, 'tile', down)  17.6 us
    all_to_all x1, blocking collectives, local(): lax.all_to_all(analysed.reshape(16, 32, 128), 'member', split_axis=0, con...  13.9 us
    ppermute x1, waiting for transfers between devices, local(): before = lax.ppermute(own, 'tile', up)  5.9 us
    ppermute x1, starting transfers between devices, local(): after = lax.ppermute(own, 'tile', down)  5.79 us
    pallas_call x1, Pallas kernels, local(): pl.pallas_call(forecast_kernel, out_shape=shape(512), in_specs=[VMEM] * 6...  3.67 us
    unnamed x18, local copies, waits for them, and re-layouts  3.19 us
    pallas_call x1, Pallas kernels, local(): pl.pallas_call(analysis_kernel, out_shape=shape(512), in_specs=[VMEM] * 7...  2.74 us
  transfers between devices with their start and end apart: 4, of which 2 were waited for; matrix products, arithmetic and copies ran while one was open for 0% of the time, Pallas kernels for 1%

profile of v1, /device:TPU:2, one launch (start us, length us, event | category | flops | bytes accessed | tf_op | source)
XLA Modules:
  0.0 78.8 jit_solution(7656731771556109917)
XLA Ops:
  0.0 0.9 %copy-done = bf16[8,4,16,128]{3,2,1,0:T(8,128)(2,1)S(1)} copy-done((bf16[8,4,16,128]{3,2,1,0:T(8,128)(2,1)S(1)}, bf16[8,4,16,128]{3,2,1,0:T(8,128)(2,1)}, u32[]{:S(2)}) %copy-start) | copy-done | bytes 131096
  0.9 0.1 edges.1
  1.0 0.0 copy-start.3
  1.0 2.1 %collective-permute-start = (bf16[96,128]{1,0:T(8,128)(2,1)S(1)}, bf16[96,128]{1,0:T(8,128)(2,1)S(1)}, u32[]{:S(2)}, u32[]{:S(2)}) collective-permute-start(bf16[96,128]{1,0:T(8,128)(2,1)S(1)} %get-tuple-element.10), channel_id=1, source_target_pairs={{0,1},{1,2},{2,3},{3,4},{4,5},{5,6},{6,7},{7,8},{8,9},{9,10},{10,1... | collective-permute-start | bytes 73736 | tf_op jit(solution)/shard_map/ppermute | solution.py:232
  3.0 17.6 %collective-permute-start.1 = (bf16[96,128]{1,0:T(8,128)(2,1)S(1)}, bf16[96,128]{1,0:T(8,128)(2,1)S(1)}, u32[]{:S(2)}, u32[]{:S(2)}) collective-permute-start(bf16[96,128]{1,0:T(8,128)(2,1)S(1)} %get-tuple-element.11), channel_id=1, source_target_pairs={{1,0},{2,1},{3,2},{4,3},{5,4},{6,5},{7,6},{8,7},{9,8},{10,9},{11,1... | collective-permute-start | bytes 73736 | tf_op jit(solution)/shard_map/ppermute | solution.py:233
  20.7 0.0 copy-start.2
  20.7 0.9 %copy-done.2 = bf16[1,32,32,3,3]{2,1,4,3,0:T(8,128)(2,1)S(1)} copy-done((bf16[1,32,32,3,3]{2,1,4,3,0:T(8,128)(2,1)S(1)}, bf16[1,32,32,3,3]{2,1,4,3,0:T(8,128)(2,1)}, u32[]{:S(2)}) %copy-start.2) | copy-done | bytes 18456
  21.6 0.7 copy-done.4
  22.3 0.4 weights.1
  22.7 0.0 collective-permute-done.above_ref
  22.7 0.0 collective-permute-done.1.below_ref
  22.8 3.7 %forecast.1 = bf16[512,128]{1,0:T(8,128)(2,1)S(1)} custom-call(bf16[512,128]{1,0:T(8,128)(2,1)S(1)} %bitcast.27, bf16[96,128]{1,0:T(8,128)(2,1)S(1)} %collective-permute-done.above_ref, bf16[96,128]{1,0:T(8,128)(2,1)S(1)} %collective-permute-done.1.below_ref, bf16[320,192]{1,0:T(8,128)(2,1)S(1)} %get-tuple-element.12.t1_ref, ...), custom_call_target="tpu_custom_call" | custom-call | tf_op jit(solution)/shard_map/forecast/pallas_call | solution.py:247
  26.4 0.0 copy-start.7
  26.4 0.0 copy-start.8
  26.5 20.0 %all_to_all.10 = bf16[16,32,128]{2,1,0:T(8,128)(2,1)S(1)} all-to-all(bf16[16,32,128]{2,1,0:T(8,128)(2,1)S(1)} %bitcast.28), channel_id=1, replica_groups=mesh['member'=16,'tile'=64] {'member'}, dimensions={0} | all-to-all | bytes 262144 | tf_op jit(solution)/shard_map/all_to_all | solution.py:262
  46.4 5.8 %collective-permute-start.3 = (bf16[512,128]{1,0:T(8,128)(2,1)S(1)}, bf16[512,128]{1,0:T(8,128)(2,1)S(1)}, u32[]{:S(2)}, u32[]{:S(2)}) collective-permute-start(bf16[512,128]{1,0:T(8,128)(2,1)S(1)} %bitcast.22), channel_id=1, source_target_pairs={{1,0},{2,1},{3,2},{4,3},{5,4},{6,5},{7,6},{8,7},{9,8},{10,9},{11,1... | collective-permute-start | bytes 393224 | tf_op jit(solution)/shard_map/ppermute | solution.py:266
  52.2 1.9 %collective-permute-start.2 = (bf16[512,128]{1,0:T(8,128)(2,1)S(1)}, bf16[512,128]{1,0:T(8,128)(2,1)S(1)}, u32[]{:S(2)}, u32[]{:S(2)}) collective-permute-start(bf16[512,128]{1,0:T(8,128)(2,1)S(1)} %bitcast.23), channel_id=1, source_target_pairs={{0,1},{1,2},{2,3},{3,4},{4,5},{5,6},{6,7},{7,8},{8,9},{9,10},{10,1... | collective-permute-start | bytes 393224 | tf_op jit(solution)/shard_map/ppermute | solution.py:265
  54.2 0.6 collective-permute-done.3.below_ref
  54.8 5.9 %collective-permute-done.2.above_ref = bf16[512,128]{1,0:T(8,128)(2,1)S(1)} collective-permute-done((bf16[512,128]{1,0:T(8,128)(2,1)S(1)}, bf16[512,128]{1,0:T(8,128)(2,1)S(1)}, u32[]{:S(2)}, u32[]{:S(2)}) %collective-permute-start.2) | collective-permute-done | bytes 131104 | tf_op jit(solution)/shard_map/ppermute | solution.py:265
  60.7 0.7 copy-done.6
  61.3 0.0 copy-done.5
  61.3 2.7 %analysis.1 = bf16[512,128]{1,0:T(8,128)(2,1)S(1)} custom-call(bf16[512,128]{1,0:T(8,128)(2,1)S(1)} %collective-permute-done.2.above_ref, bf16[512,128]{1,0:T(8,128)(2,1)S(1)} %bitcast.24, bf16[512,128]{1,0:T(8,128)(2,1)S(1)} %collective-permute-done.3.below_ref, f32[1,512]{1,0:T(1,128)S(1)} %bitcast.32, f32[1,512]{1,0:T(1,128)S(1)} %bitcast.33, ...), custom_call_target="tpu_custom_call" | custom-call | tf_op jit(solution)/shard_map/analysis/pallas_call | solution.py:267
  64.1 13.9 %all_to_all.11 = bf16[16,32,128]{2,1,0:T(8,128)(2,1)S(1)} all-to-all(bf16[16,32,128]{2,1,0:T(8,128)(2,1)S(1)} %bitcast.25), channel_id=1, replica_groups=mesh['member'=16,'tile'=64] {'member'}, dimensions={0} | all-to-all | bytes 262144 | tf_op jit(solution)/shard_map/all_to_all | solution.py:284
  77.9 0.8 %unpack.1 = bf16[512,128]{1,0:T(8,128)(2,1)} custom-call(bf16[512,128]{1,0:T(8,128)(2,1)S(1)} %bitcast.21), custom_call_target="tpu_custom_call" | custom-call | tf_op jit(solution)/shard_map/unpack/pallas_call | solution.py:287
  (9 shorter events, 0.0 us)
Async XLA Ops:
  0.0 0.9 %copy-start = (bf16[8,4,16,128]{3,2,1,0:T(8,128)(2,1)S(1)}, bf16[8,4,16,128]{3,2,1,0:T(8,128)(2,1)}, u32[]{:S(2)}) copy-start(bf16[8,4,16,128]{3,2,1,0:T(8,128)(2,1)} %param.8) | copy-start | bytes 393220
  0.9 21.8 %copy-start.1 = (bf16[8,4,16,128]{3,2,1,0:T(8,128)(2,1)S(1)}, bf16[8,4,16,128]{3,2,1,0:T(8,128)(2,1)}, u32[]{:S(2)}) copy-start(bf16[8,4,16,128]{3,2,1,0:T(8,128)(2,1)} %param.8) | copy-start | bytes 393220
  1.0 19.7 %copy-start.3 = (bf16[32,4,3,3]{0,1,3,2:T(4,128)(2,1)S(1)}, bf16[32,4,3,3]{0,1,3,2:T(4,128)(2,1)}, u32[]{:S(2)}) copy-start(bf16[32,4,3,3]{0,1,3,2:T(4,128)(2,1)} %param.9) | copy-start | bytes 6916
  1.0 21.8 %collective-permute-start = (bf16[96,128]{1,0:T(8,128)(2,1)S(1)}, bf16[96,128]{1,0:T(8,128)(2,1)S(1)}, u32[]{:S(2)}, u32[]{:S(2)}) collective-permute-start(bf16[96,128]{1,0:T(8,128)(2,1)S(1)} %get-tuple-element.10), channel_id=1, source_target_pairs={{0,1},{1,2},{2,3},{3,4},{4,5},{5,6},{6,7},{7,8},{8,9},{9,10},{10,1... | collective-permute-start | bytes 73736 | tf_op jit(solution)/shard_map/ppermute | solution.py:232
  3.0 19.7 %collective-permute-start.1 = (bf16[96,128]{1,0:T(8,128)(2,1)S(1)}, bf16[96,128]{1,0:T(8,128)(2,1)S(1)}, u32[]{:S(2)}, u32[]{:S(2)}) collective-permute-start(bf16[96,128]{1,0:T(8,128)(2,1)S(1)} %get-tuple-element.11), channel_id=1, source_target_pairs={{1,0},{2,1},{3,2},{4,3},{5,4},{6,5},{7,6},{8,7},{9,8},{10,9},{11,1... | collective-permute-start | bytes 73736 | tf_op jit(solution)/shard_map/ppermute | solution.py:233
  20.7 0.9 %copy-start.2 = (bf16[1,32,32,3,3]{2,1,4,3,0:T(8,128)(2,1)S(1)}, bf16[1,32,32,3,3]{2,1,4,3,0:T(8,128)(2,1)}, u32[]{:S(2)}) copy-start(bf16[1,32,32,3,3]{2,1,4,3,0:T(8,128)(2,1)} %param.10) | copy-start | bytes 55300
  21.6 0.7 copy-start.4
  26.4 34.2 %copy-start.7 = (s32[1,1,512]{2,1,0:T(1,128)S(1)}, s32[1,1,512]{2,1,0:T(1,128)}, u32[]{:S(2)}) copy-start(s32[1,1,512]{2,1,0:T(1,128)} %param.14) | copy-start | bytes 6148
  26.4 34.2 %copy-start.8 = (s32[1,1,512]{2,1,0:T(1,128)S(1)}, s32[1,1,512]{2,1,0:T(1,128)}, u32[]{:S(2)}) copy-start(s32[1,1,512]{2,1,0:T(1,128)} %param.15) | copy-start | bytes 6148
  46.4 8.3 %collective-permute-start.3 = (bf16[512,128]{1,0:T(8,128)(2,1)S(1)}, bf16[512,128]{1,0:T(8,128)(2,1)S(1)}, u32[]{:S(2)}, u32[]{:S(2)}) collective-permute-start(bf16[512,128]{1,0:T(8,128)(2,1)S(1)} %bitcast.22), channel_id=1, source_target_pairs={{1,0},{2,1},{3,2},{4,3},{5,4},{6,5},{7,6},{8,7},{9,8},{10,9},{11,1... | collective-permute-start | bytes 393224 | tf_op jit(solution)/shard_map/ppermute | solution.py:266
  52.2 8.4 %collective-permute-start.2 = (bf16[512,128]{1,0:T(8,128)(2,1)S(1)}, bf16[512,128]{1,0:T(8,128)(2,1)S(1)}, u32[]{:S(2)}, u32[]{:S(2)}) collective-permute-start(bf16[512,128]{1,0:T(8,128)(2,1)S(1)} %bitcast.23), channel_id=1, source_target_pairs={{0,1},{1,2},{2,3},{3,4},{4,5},{5,6},{6,7},{7,8},{8,9},{9,10},{10,1... | collective-permute-start | bytes 393224 | tf_op jit(solution)/shard_map/ppermute | solution.py:265
  60.6 0.7 copy-start.6
  60.6 0.7 copy-start.5

commit v2 on v1

v2 whole, which is shorter than its diff:
```python
import jax
import jax.numpy as jnp
from jax import lax
from jax.experimental import pallas as pl
from jax.experimental.pallas import tpu as pltpu
from jax.sharding import PartitionSpec as P

NS_ITERS = 4
F32 = jnp.float32
BF16 = jnp.bfloat16
VMEM = pl.BlockSpec(memory_space=pltpu.VMEM)


def params(mib):
    return pltpu.CompilerParams(vmem_limit_bytes=mib << 20)


def silu(v):
    half = 0.5 * v
    return half + half * jnp.tanh(half)


def iota(shape, axis):
    return lax.broadcasted_iota(jnp.int32, shape, axis)


def pick(distance, choices):
    out = jnp.zeros(distance.shape, F32)
    for tap, value in enumerate(choices):
        out = jnp.where(distance == tap, value, out)
    return out


def edges_kernel(*refs):
    sources, (near_ref, far_ref), targets, (wide, arrived) = refs[:8], refs[8:10], refs[10:18], refs[18:]
    odd = lax.axis_index("tile") % 2
    copies = [
        pltpu.make_async_copy(source, target, arrived.at[number])
        for number, (source, target) in enumerate(zip(sources, targets))
    ]
    for copy in copies:
        copy.start()
    copies[0].wait()
    wide[...] = targets[0][...].astype(F32)
    for row in range(3):
        place = slice(row * 32, (row + 1) * 32)
        near_ref[place, :] = wide[pl.ds(13 * (1 - odd) + row, 32, stride=16), :].astype(BF16)
        far_ref[place, :] = wide[pl.ds(13 * odd + row, 32, stride=16), :].astype(BF16)
    for copy in copies[1:]:
        copy.wait()


def weights_kernel(first_ref, middle_ref, last_ref, t1_ref, t2_ref, t3_ref):
    where_to = iota((4, 192), 1) // 16
    expanded = []
    for dy in range(3):
        total = jnp.zeros((32, 192), F32)
        for dx in range(3):
            spread = (where_to == iota((4, 192), 0) + 4 * dx).astype(BF16)
            total += lax.dot_general(
                first_ref[dy * 3 + dx], spread, (((0,), (0,)), ((), ())), preferred_element_type=F32
            )
        expanded.append(jnp.concatenate([total] * 10, axis=0))
    distance = iota((320, 192), 1) % 16 - iota((320, 192), 0) // 32
    t1_ref[...] = pick(distance, expanded).astype(BF16)
    distance = iota((192, 256), 1) // 32 - iota((192, 256), 0) // 32
    for dx in range(3):
        taps = []
        for dy in range(3):
            one = middle_ref[dy * 3 + dx].astype(F32)
            wide = jnp.concatenate([one] * 8, axis=1)
            taps.append(jnp.concatenate([wide] * 6, axis=0))
        t2_ref[dx * 192 : (dx + 1) * 192, :] = pick(distance, taps).astype(BF16)
    distance = iota((64, 640), 1) // 32 - iota((64, 640), 0) % 16
    for dx in range(3):
        taps = []
        for dy in range(3):
            one = last_ref[dy * 3 + dx].astype(F32)
            wide = jnp.concatenate([one] * 4, axis=1)
            rows = jnp.concatenate(
                [jnp.broadcast_to(wide[f : f + 1], (16, 128)) for f in range(4)], axis=0
            )
            taps.append(jnp.concatenate([rows] * 5, axis=1))
        t3_ref[dx * 64 : (dx + 1) * 64, :] = pick(distance, taps).astype(BF16)[:, :576]


def forecast_kernel(
    state_ref, near_ref, far_ref, t1_ref, t2_ref, t3_ref, out_ref, wide, padded, h1, h2, sent
):
    odd = lax.axis_index("tile") % 2
    wide[...] = state_ref[...].astype(F32)
    nothing = jnp.zeros((32, 128), F32)
    for row in range(16):
        if 3 <= row < 12:
            padded[pl.ds(row, 32, stride=16), :] = wide[pl.ds(row - 3, 32, stride=16), :]
        if row < 9:
            padded[pl.ds(512 + row, 32, stride=16), :] = wide[pl.ds(row + 7, 32, stride=16), :]
        if row >= 12:
            padded[pl.ds(row, 32, stride=16), :] = nothing
            padded[pl.ds(512 + row, 32, stride=16), :] = nothing
    for row in range(3):
        place = slice(row * 32, (row + 1) * 32)
        near_at, far_at = 521 * (1 - odd) + row, 521 * odd + row
        padded[pl.ds(near_at, 32, stride=16), :] = near_ref[place, :].astype(F32)
        padded[pl.ds(far_at, 32, stride=16), :] = far_ref[place, :].astype(F32)

    def lanes(side):
        return slice(side * 128, (side + 1) * 128)

    def joined(taps, side, rows):
        part = taps[:, lanes(side)]
        return (
            part[rows : 2 * rows]
            + pltpu.roll(part[:rows], 1, 1)
            + pltpu.roll(part[2 * rows :], 127, 1)
        )

    def first(pair, half):
        sides = []
        for member in (2 * pair, 2 * pair + 1):
            start = half * 512 + member * 64
            rows = padded[start : start + 64, :]
            sides.append(
                jnp.concatenate([pltpu.roll(rows, 1, 1), rows, pltpu.roll(rows, 127, 1)], axis=0)
            )
        columns = jnp.concatenate(sides, axis=1).astype(BF16)
        summed = jnp.dot(t1_ref[...], columns, preferred_element_type=F32)
        yield
        h1[pair, half * 320 : (half + 1) * 320, :] = silu(summed).astype(BF16)

    def second(pair, group):
        columns = h1[pair, group * 192 : group * 192 + 256, :]
        taps = jnp.dot(t2_ref[...], columns, preferred_element_type=F32)
        yield
        for side in range(2):
            h2[pair, group * 192 : (group + 1) * 192, lanes(side)] = silu(
                joined(taps, side, 192)
            ).astype(BF16)

    def third(pair):
        taps = jnp.dot(t3_ref[...], h2[pair], preferred_element_type=F32)
        yield
        for side in range(2):
            member = 2 * pair + side
            result = wide[member * 64 : (member + 1) * 64, :] + joined(taps, side, 64)
            for f in range(4):
                sent[pl.ds(f * 8 + member, 16, stride=32), :] = result[f * 16 : (f + 1) * 16]

    order = []
    for pairs in ((0, 1), (2, 3)):
        order += [first(pair, half) for half in range(2) for pair in pairs]
        order += [second(pair, group) for group in range(3) for pair in pairs]
        order += [third(pair) for pair in pairs]
    pending = []
    for task in order:
        next(task)
        pending.append(task)
        if len(pending) > 1:
            next(pending.pop(0), None)
    for task in pending:
        next(task, None)
    out_ref[...] = sent[...].astype(BF16)


def split(value):
    high = value.astype(BF16)
    return high, (value - high.astype(F32)).astype(BF16)


def fine_dot(a, b, contract=((1,), (0,))):
    (a_high, a_low), (b_high, b_low) = a, b

    def one(left, right):
        return lax.dot_general(left, right, (contract, ((), ())), preferred_element_type=F32)

    return one(a_high, b_high) + (one(a_high, b_low) + one(a_low, b_high))


def members_by_points(ref):
    blocks = ref[...].astype(F32).reshape(16, 4, 8, 128)
    return jnp.concatenate([blocks[:, f].reshape(128, 128) for f in range(4)], axis=1)


def observe_kernel(rows_ref, hot_ref):
    picked = rows_ref[...]
    entry = iota((256, 512), 0)
    for part in range(6):
        hot_ref[part * 256 : (part + 1) * 256, :] = (
            (entry == picked - part * 256).astype(F32).astype(BF16)
        )


def own_kernel(own_ref, hot_ref, ens_ref, shift_ref, high_ref, low_ref):
    back = members_by_points(own_ref)
    ens_ref[...] = jnp.dot(
        back.astype(BF16), hot_ref[512:1024, :], preferred_element_type=F32
    )
    mean = jnp.sum(back, axis=0, keepdims=True) * (1.0 / 128)
    shift_ref[...] = mean
    high, low = split(back - mean)
    high_ref[...] = high
    low_ref[...] = low


def analysis_kernel(
    near_ref,
    far_ref,
    hot_ref,
    ens_ref,
    shift_ref,
    high_ref,
    low_ref,
    obs_ref,
    var_ref,
    class_ref,
    out_ref,
    held,
):
    size = 128
    odd = lax.axis_index("tile") % 2
    obs_ens = ens_ref[...]
    for ref, start in ((near_ref, 1024 * (1 - odd)), (far_ref, 1024 * odd)):
        chosen = hot_ref[pl.ds(pl.multiple_of(start, 512), 512), :]
        obs_ens += jnp.dot(
            members_by_points(ref).astype(BF16), chosen, preferred_element_type=F32
        )
    obs_mean = jnp.sum(obs_ens, axis=0, keepdims=True) * (1.0 / size)
    anom = obs_ens - obs_mean
    weight = jnp.exp(-0.25 * class_ref[...].astype(F32)) / var_ref[...]
    identity = (iota((size, size), 0) == iota((size, size), 1)).astype(F32)
    gram = (size - 1.0) * identity + fine_dot(split(anom), split(anom * weight), ((1,), (1,)))
    residual = jnp.sum(anom * (weight * (obs_ref[...] - obs_mean)), axis=1, keepdims=True)
    square = jnp.sum(jnp.sum(gram * gram, axis=1, keepdims=True), axis=0, keepdims=True)
    norm = jnp.sqrt(square)
    y = gram * (1.0 / norm)
    z = 1.5 * identity - 0.5 * y
    y_parts, z_parts = split(y), split(z)
    y_parts = split(fine_dot(y_parts, z_parts))
    for sweep in range(1, NS_ITERS):
        factor = split(1.5 * identity - 0.5 * fine_dot(z_parts, y_parts))
        if sweep + 1 < NS_ITERS:
            y_parts = split(fine_dot(y_parts, factor))
        z = fine_dot(factor, z_parts)
        z_parts = split(z)
    root = z * (1.0 / jnp.sqrt(norm))
    once = jnp.sum(root * residual, axis=0, keepdims=True)
    mean_weights = jnp.sum(root * once, axis=1, keepdims=True)
    high, low = high_ref[...], low_ref[...]
    anomaly = high.astype(F32) + low.astype(F32)
    shift = shift_ref[...] + jnp.sum(mean_weights * anomaly, axis=0, keepdims=True)
    result = shift + fine_dot(split(root * (size - 1.0) ** 0.5), (high, low))
    for f in range(4):
        held[:, f] = result[:, f * 128 : (f + 1) * 128].reshape(16, 8, 128)
    out_ref[...] = held[...].reshape(512, 128).astype(BF16)


def unpack_kernel(in_ref, out_ref, wide):
    wide[...] = in_ref[...].astype(F32)
    for lane in range(32):
        member, f = lane // 4, lane % 4
        out_ref[lane * 16 : (lane + 1) * 16, :] = wide[
            pl.ds(f * 8 + member, 16, stride=32), :
        ].astype(BF16)


def shape(rows, columns=128):
    return jax.ShapeDtypeStruct((rows, columns), BF16)


def scratch(*dims, dtype=F32):
    return pltpu.VMEM(dims, dtype)


def local(
    state,
    first_weight,
    middle_weight,
    last_weight,
    observations,
    obs_variance,
    observation_rows,
    loc_class,
):
    count = lax.axis_size("tile")
    near = [(i, i ^ 1) for i in range(count)]
    far = [(i, (i + (1 if i % 2 else -1)) % count) for i in range(count)]
    given = (
        state.reshape(512, 128),
        jnp.transpose(first_weight, (2, 3, 1, 0)).reshape(9, 4, 32),
        jnp.transpose(middle_weight[0], (2, 3, 0, 1)).reshape(9, 32, 32),
        jnp.transpose(last_weight, (2, 3, 0, 1)).reshape(9, 4, 32),
        observations.reshape(1, 512),
        obs_variance.reshape(1, 512),
        observation_rows.reshape(1, 512),
        loc_class.reshape(1, 512),
    )
    near_edge, far_edge, rows, first, middle, last, obs, variance, read, classes = pl.pallas_call(
        edges_kernel,
        out_shape=(shape(96), shape(96))
        + tuple(jax.ShapeDtypeStruct(a.shape, a.dtype) for a in given),
        in_specs=[pl.BlockSpec(memory_space=pltpu.HBM)] * 8,
        out_specs=(VMEM,) * 10,
        scratch_shapes=[scratch(512, 128), pltpu.SemaphoreType.DMA((8,))],
        compiler_params=params(8),
        name="edges",
    )(*(pltpu.with_memory_space_constraint(a, pltpu.HBM) for a in given))
    from_far = lax.ppermute(far_edge, "tile", far)
    from_near = lax.ppermute(near_edge, "tile", near)
    t1, t2, t3 = pl.pallas_call(
        weights_kernel,
        out_shape=(shape(320, 192), shape(576, 256), shape(192, 576)),
        in_specs=[VMEM] * 3,
        out_specs=(VMEM,) * 3,
        compiler_params=params(8),
        cost_estimate=pl.CostEstimate(flops=4000000, bytes_accessed=700000, transcendentals=0),
        name="weights",
    )(first, middle, last)
    forecast = pl.pallas_call(
        forecast_kernel,
        out_shape=shape(512),
        in_specs=[VMEM] * 6,
        out_specs=VMEM,
        scratch_shapes=[
            scratch(512, 128),
            scratch(1024, 128),
            scratch(4, 640, 256, dtype=BF16),
            scratch(4, 576, 256, dtype=BF16),
            scratch(512, 128),
        ],
        compiler_params=params(16),
        name="forecast",
    )(rows, from_near, from_far, t1, t2, t3)
    own = lax.all_to_all(
        forecast.reshape(16, 32, 128), "member", split_axis=0, concat_axis=0, tiled=True
    ).reshape(512, 128)
    hot = pl.pallas_call(
        observe_kernel,
        out_shape=shape(1536, 512),
        in_specs=[VMEM],
        out_specs=VMEM,
        compiler_params=params(8),
        cost_estimate=pl.CostEstimate(flops=4000000, bytes_accessed=1600000, transcendentals=0),
        name="observe",
    )(read)
    from_far = lax.ppermute(own, "tile", far)
    from_near = lax.ppermute(own, "tile", near)
    ens, mean, high, low = pl.pallas_call(
        own_kernel,
        out_shape=(
            jax.ShapeDtypeStruct((128, 512), F32),
            jax.ShapeDtypeStruct((1, 512), F32),
            shape(128, 512),
            shape(128, 512),
        ),
        in_specs=[VMEM] * 2,
        out_specs=(VMEM,) * 4,
        compiler_params=params(8),
        cost_estimate=pl.CostEstimate(flops=70000000, bytes_accessed=1200000, transcendentals=0),
        name="own",
    )(own, hot)
    analysed = pl.pallas_call(
        analysis_kernel,
        out_shape=shape(512),
        in_specs=[VMEM] * 10,
        out_specs=VMEM,
        scratch_shapes=[scratch(16, 4, 8, 128)],
        compiler_params=params(16),
        name="analysis",
    )(from_near, from_far, hot, ens, mean, high, low, obs, variance, classes)
    returned = lax.all_to_all(
        analysed.reshape(16, 32, 128), "member", split_axis=0, concat_axis=0, tiled=True
    ).reshape(512, 128)
    out = pl.pallas_call(
        unpack_kernel,
        out_shape=shape(512),
        in_specs=[VMEM],
        out_specs=VMEM,
        scratch_shapes=[scratch(512, 128)],
        compiler_params=params(8),
        name="unpack",
    )(returned)
    return out.reshape(8, 4, 16, 128)


def solution(mesh):
    return jax.shard_map(
        local,
        mesh=mesh,
        in_specs=(
            P("member", None, "tile", None),
            P(),
            P(),
            P(),
            P("tile", "member", None),
            P("tile", "member", None),
            P("tile", "member", None),
            P("tile", "member", None),
        ),
        out_specs=P("member", None, "tile", None),
        check_vma=False,
    )
```

time: 79.2 us -> 72.1 us (0.910)
  waiting for transfers between devices: 6.47 us -> 1.99 us
  local copies, waits for them, and re-layouts: 3.19 us -> 0 us
    ppermute x4, waiting for transfers between devices: 6.47 us -> 1.99 us  [the longest x1 1.04 us: local(): from_far = lax.ppermute(far_edge, 'tile', far)]
    unnamed x18 -> x0, local copies, waits for them, and re-layouts: 3.19 us -> none
    pallas_call x2 -> x4, Pallas kernels: 2.79 us -> 3.83 us  [the longest x1 2.27 us: local(): pl.pallas_call(analysis_kernel, out_shape=shape(512), in_specs=[VMEM] * 1...]
where the time goes in v2:
time: 72.1 us; the launch traced here: 71.8 us
  blocking collectives  34.2 us (47%)
  starting transfers between devices  27.1 us (38%)
  Pallas kernels  8.41 us (12%)
  waiting for transfers between devices  1.99 us (3%)
    all_to_all x1, blocking collectives, local(): lax.all_to_all(forecast.reshape(16, 32, 128), 'member', split_axis=0, con...  20 us
    ppermute x1, starting transfers between devices, local(): from_far = lax.ppermute(far_edge, 'tile', far)  18.3 us
    all_to_all x1, blocking collectives, local(): lax.all_to_all(analysed.reshape(16, 32, 128), 'member', split_axis=0, con...  14.3 us
    ppermute x1, starting transfers between devices, local(): from_far = lax.ppermute(own, 'tile', far)  4.97 us
    pallas_call x1, Pallas kernels, local(): pl.pallas_call(forecast_kernel, out_shape=shape(512), in_specs=[VMEM] * 6...  3.32 us
    pallas_call x1, Pallas kernels, local(): pl.pallas_call(analysis_kernel, out_shape=shape(512), in_specs=[VMEM] * 1...  2.27 us
    ppermute x1, starting transfers between devices, local(): from_near = lax.ppermute(near_edge, 'tile', near)  1.92 us
    ppermute x1, starting transfers between devices, local(): from_near = lax.ppermute(own, 'tile', near)  1.92 us
  transfers between devices with their start and end apart: 4, of which 2 were waited for; matrix products, arithmetic and copies ran while one was open for 0% of the time, Pallas kernels for 1%

profile of v2, /device:TPU:2, one launch (start us, length us, event | category | flops | bytes accessed | tf_op | source)
XLA Modules:
  0.0 71.8 jit_solution(10135840736533329566)
XLA Ops:
  0.0 1.0 %edges.1 = (bf16[96,128]{1,0:T(8,128)(2,1)S(1)}, bf16[96,128]{1,0:T(8,128)(2,1)S(1)}, bf16[512,128]{1,0:T(8,128)(2,1)S(1)}, bf16[9,4,32]{2,1,0:T(4,128)(2,1)S(1)...) custom-call(bf16[512,128]{1,0:T(8,128)(2,1)} %bitcast.27, ...), custom_call_target="tpu_custom_call" | custom-call | tf_op jit(solution)/shard_map/edges/pallas_call | solution.py:297
  1.1 1.9 %collective-permute-start = (bf16[96,128]{1,0:T(8,128)(2,1)S(1)}, bf16[96,128]{1,0:T(8,128)(2,1)S(1)}, u32[]{:S(2)}, u32[]{:S(2)}) collective-permute-start(bf16[96,128]{1,0:T(8,128)(2,1)S(1)} %get-tuple-element.23), channel_id=1, source_target_pairs={{0,1},{1,0},{2,3},{3,2},{4,5},{5,4},{6,7},{7,6},{8,9},{9,8},{10,11... | collective-permute-start | bytes 73736 | tf_op jit(solution)/shard_map/ppermute | solution.py:308
  3.0 18.3 %collective-permute-start.1 = (bf16[96,128]{1,0:T(8,128)(2,1)S(1)}, bf16[96,128]{1,0:T(8,128)(2,1)S(1)}, u32[]{:S(2)}, u32[]{:S(2)}) collective-permute-start(bf16[96,128]{1,0:T(8,128)(2,1)S(1)} %get-tuple-element.24), channel_id=1, source_target_pairs={{0,63},{1,2},{2,1},{3,4},{4,3},{5,6},{6,5},{7,8},{8,7},{9,10},{10,... | collective-permute-start | bytes 73736 | tf_op jit(solution)/shard_map/ppermute | solution.py:307
  21.3 0.4 weights.1
  21.7 0.0 collective-permute-done.near_ref
  21.7 1.0 %collective-permute-done.1.far_ref = bf16[96,128]{1,0:T(8,128)(2,1)S(1)} collective-permute-done((bf16[96,128]{1,0:T(8,128)(2,1)S(1)}, bf16[96,128]{1,0:T(8,128)(2,1)S(1)}, u32[]{:S(2)}, u32[]{:S(2)}) %collective-permute-start.1) | collective-permute-done | bytes 24608 | tf_op jit(solution)/shard_map/ppermute | solution.py:307
  22.8 3.3 %forecast.1 = bf16[512,128]{1,0:T(8,128)(2,1)S(1)} custom-call(bf16[512,128]{1,0:T(8,128)(2,1)S(1)} %get-tuple-element.22.state_ref, bf16[96,128]{1,0:T(8,128)(2,1)S(1)} %collective-permute-done.near_ref, bf16[96,128]{1,0:T(8,128)(2,1)S(1)} %collective-permute-done.1.far_ref, bf16[320,192]{1,0:T(8,128)(2,1)S(1)} %get-tuple-element.28.t1_ref, ...), custom_call_target="tpu_custom_call" | custom-call | tf_op jit(solution)/shard_map/forecast/pallas_call | solution.py:318
  26.1 20.0 %all_to_all.10 = bf16[16,32,128]{2,1,0:T(8,128)(2,1)S(1)} all-to-all(bf16[16,32,128]{2,1,0:T(8,128)(2,1)S(1)} %bitcast.26), channel_id=1, replica_groups=mesh['member'=16,'tile'=64] {'member'}, dimensions={0} | all-to-all | bytes 262144 | tf_op jit(solution)/shard_map/all_to_all | solution.py:333
  46.1 5.0 %collective-permute-start.3 = (bf16[512,128]{1,0:T(8,128)(2,1)S(1)}, bf16[512,128]{1,0:T(8,128)(2,1)S(1)}, u32[]{:S(2)}, u32[]{:S(2)}) collective-permute-start(bf16[512,128]{1,0:T(8,128)(2,1)S(1)} %bitcast.23), channel_id=1, source_target_pairs={{0,63},{1,2},{2,1},{3,4},{4,3},{5,6},{6,5},{7,8},{8,7},{9,10},{10,... | collective-permute-start | bytes 393224 | tf_op jit(solution)/shard_map/ppermute | solution.py:345
  51.1 1.9 %collective-permute-start.2 = (bf16[512,128]{1,0:T(8,128)(2,1)S(1)}, bf16[512,128]{1,0:T(8,128)(2,1)S(1)}, u32[]{:S(2)}, u32[]{:S(2)}) collective-permute-start(bf16[512,128]{1,0:T(8,128)(2,1)S(1)} %bitcast.24), channel_id=1, source_target_pairs={{0,1},{1,0},{2,3},{3,2},{4,5},{5,4},{6,7},{7,6},{8,9},{9,8},{10,11... | collective-permute-start | bytes 393224 | tf_op jit(solution)/shard_map/ppermute | solution.py:346
  53.0 0.3 observe.1.hot_ref
  53.3 0.3 own.1
  53.5 1.0 %collective-permute-done.3.far_ref = bf16[512,128]{1,0:T(8,128)(2,1)S(1)} collective-permute-done((bf16[512,128]{1,0:T(8,128)(2,1)S(1)}, bf16[512,128]{1,0:T(8,128)(2,1)S(1)}, u32[]{:S(2)}, u32[]{:S(2)}) %collective-permute-start.3) | collective-permute-done | bytes 131104 | tf_op jit(solution)/shard_map/ppermute | solution.py:345
  54.5 0.0 collective-permute-done.2.near_ref
  54.5 2.3 %analysis.1 = bf16[512,128]{1,0:T(8,128)(2,1)S(1)} custom-call(bf16[512,128]{1,0:T(8,128)(2,1)S(1)} %collective-permute-done.2.near_ref, bf16[512,128]{1,0:T(8,128)(2,1)S(1)} %collective-permute-done.3.far_ref, bf16[1536,512]{1,0:T(8,128)(2,1)S(1)} %observe.1.hot_ref, f32[128,512]{1,0:T(8,128)S(1)} %get-tuple-element.32.ens_ref, ...), custom_call_target="tpu_custom_call" | custom-call | tf_op jit(solution)/shard_map/analysis/pallas_call | solution.py:361
  56.8 14.3 %all_to_all.11 = bf16[16,32,128]{2,1,0:T(8,128)(2,1)S(1)} all-to-all(bf16[16,32,128]{2,1,0:T(8,128)(2,1)S(1)} %bitcast.21), channel_id=1, replica_groups=mesh['member'=16,'tile'=64] {'member'}, dimensions={0} | all-to-all | bytes 262144 | tf_op jit(solution)/shard_map/all_to_all | solution.py:370
  71.0 0.8 %unpack.1 = bf16[512,128]{1,0:T(8,128)(2,1)} custom-call(bf16[512,128]{1,0:T(8,128)(2,1)S(1)} %bitcast.22), custom_call_target="tpu_custom_call" | custom-call | tf_op jit(solution)/shard_map/unpack/pallas_call | solution.py:373
Async XLA Ops:
  1.1 20.7 %collective-permute-start = (bf16[96,128]{1,0:T(8,128)(2,1)S(1)}, bf16[96,128]{1,0:T(8,128)(2,1)S(1)}, u32[]{:S(2)}, u32[]{:S(2)}) collective-permute-start(bf16[96,128]{1,0:T(8,128)(2,1)S(1)} %get-tuple-element.23), channel_id=1, source_target_pairs={{0,1},{1,0},{2,3},{3,2},{4,5},{5,4},{6,7},{7,6},{8,9},{9,8},{10,11... | collective-permute-start | bytes 73736 | tf_op jit(solution)/shard_map/ppermute | solution.py:308
  3.0 19.8 %collective-permute-start.1 = (bf16[96,128]{1,0:T(8,128)(2,1)S(1)}, bf16[96,128]{1,0:T(8,128)(2,1)S(1)}, u32[]{:S(2)}, u32[]{:S(2)}) collective-permute-start(bf16[96,128]{1,0:T(8,128)(2,1)S(1)} %get-tuple-element.24), channel_id=1, source_target_pairs={{0,63},{1,2},{2,1},{3,4},{4,3},{5,6},{6,5},{7,8},{8,7},{9,10},{10,... | collective-permute-start | bytes 73736 | tf_op jit(solution)/shard_map/ppermute | solution.py:307
  46.1 8.4 %collective-permute-start.3 = (bf16[512,128]{1,0:T(8,128)(2,1)S(1)}, bf16[512,128]{1,0:T(8,128)(2,1)S(1)}, u32[]{:S(2)}, u32[]{:S(2)}) collective-permute-start(bf16[512,128]{1,0:T(8,128)(2,1)S(1)} %bitcast.23), channel_id=1, source_target_pairs={{0,63},{1,2},{2,1},{3,4},{4,3},{5,6},{6,5},{7,8},{8,7},{9,10},{10,... | collective-permute-start | bytes 393224 | tf_op jit(solution)/shard_map/ppermute | solution.py:345
  51.1 3.4 %collective-permute-start.2 = (bf16[512,128]{1,0:T(8,128)(2,1)S(1)}, bf16[512,128]{1,0:T(8,128)(2,1)S(1)}, u32[]{:S(2)}, u32[]{:S(2)}) collective-permute-start(bf16[512,128]{1,0:T(8,128)(2,1)S(1)} %bitcast.24), channel_id=1, source_target_pairs={{0,1},{1,0},{2,3},{3,2},{4,5},{5,4},{6,7},{7,6},{8,9},{9,8},{10,11... | collective-permute-start | bytes 393224 | tf_op jit(solution)/shard_map/ppermute | solution.py:346

commit v3 on v2

--- a/solution.py
+++ b/solution.py
@@ -48,6 +48,12 @@
         far_ref[place, :] = wide[pl.ds(13 * odd + row, 32, stride=16), :].astype(BF16)
     for copy in copies[1:]:
         copy.wait()
+
+
+def spread_blocks(ref, dx, value):
+    for block in range(value.shape[0] // 16):
+        start = block * 48 + dx * 16
+        ref[start : start + 16, :] = value[block * 16 : block * 16 + 16]
 
 
 def weights_kernel(first_ref, middle_ref, last_ref, t1_ref, t2_ref, t3_ref):
@@ -70,7 +76,7 @@
             one = middle_ref[dy * 3 + dx].astype(F32)
             wide = jnp.concatenate([one] * 8, axis=1)
             taps.append(jnp.concatenate([wide] * 6, axis=0))
-        t2_ref[dx * 192 : (dx + 1) * 192, :] = pick(distance, taps).astype(BF16)
+        spread_blocks(t2_ref, dx, pick(distance, taps).astype(BF16))
     distance = iota((64, 640), 1) // 32 - iota((64, 640), 0) % 16
     for dx in range(3):
         taps = []
@@ -81,7 +87,7 @@
                 [jnp.broadcast_to(wide[f : f + 1], (16, 128)) for f in range(4)], axis=0
             )
             taps.append(jnp.concatenate([rows] * 5, axis=1))
-        t3_ref[dx * 64 : (dx + 1) * 64, :] = pick(distance, taps).astype(BF16)[:, :576]
+        spread_blocks(t3_ref, dx, pick(distance, taps).astype(BF16)[:, :576])
 
 
 def forecast_kernel(
@@ -108,12 +114,9 @@
         return slice(side * 128, (side + 1) * 128)
 
     def joined(taps, side, rows):
-        part = taps[:, lanes(side)]
-        return (
-            part[rows : 2 * rows]
-            + pltpu.roll(part[:rows], 1, 1)
-            + pltpu.roll(part[2 * rows :], 127, 1)
-        )
+        part = taps[:, lanes(side)].reshape(rows // 16, 3, 16, 128)
+        left, middle, right = (part[:, dx].reshape(rows, 128) for dx in range(3))
+        return middle + pltpu.roll(left, 1, 1) + pltpu.roll(right, 127, 1)
 
     def first(pair, half):
         sides = []
@@ -147,7 +150,7 @@
                 sent[pl.ds(f * 8 + member, 16, stride=32), :] = result[f * 16 : (f + 1) * 16]
 
     order = []
-    for pairs in ((0, 1), (2, 3)):
+    for pairs in ((0, 1, 2, 3),):
         order += [first(pair, half) for half in range(2) for pair in pairs]
         order += [second(pair, group) for group in range(3) for pair in pairs]
         order += [third(pair) for pair in pairs]
@@ -155,7 +158,7 @@
     for task in order:
         next(task)
         pending.append(task)
-        if len(pending) > 1:
+        if len(pending) > 2:
             next(pending.pop(0), None)
     for task in pending:
         next(task, None)
@@ -271,6 +274,15 @@
     return pltpu.VMEM(dims, dtype)
 
 
+def exchange(near_values, far_values):
+    count = lax.axis_size("tile")
+    near = [(i, i ^ 1) for i in range(count)]
+    far = [(i, (i + (1 if i % 2 else -1)) % count) for i in range(count)]
+    from_far = lax.ppermute(far_values, "tile", far)
+    from_near = lax.ppermute(near_values, "tile", near)
+    return from_near, from_far
+
+
 def local(
     state,
     first_weight,
@@ -281,9 +293,6 @@
     observation_rows,
     loc_class,
 ):
-    count = lax.axis_size("tile")
-    near = [(i, i ^ 1) for i in range(count)]
-    far = [(i, (i + (1 if i % 2 else -1)) % count) for i in range(count)]
     given = (
         state.reshape(512, 128),
         jnp.transpose(first_weight, (2, 3, 1, 0)).reshape(9, 4, 32),
@@ -304,8 +313,7 @@
         compiler_params=params(8),
         name="edges",
     )(*(pltpu.with_memory_space_constraint(a, pltpu.HBM) for a in given))
-    from_far = lax.ppermute(far_edge, "tile", far)
-    from_near = lax.ppermute(near_edge, "tile", near)
+    from_near, from_far = exchange(near_edge, far_edge)
     t1, t2, t3 = pl.pallas_call(
         weights_kernel,
         out_shape=(shape(320, 192), shape(576, 256), shape(192, 576)),
@@ -342,8 +350,7 @@
         cost_estimate=pl.CostEstimate(flops=4000000, bytes_accessed=1600000, transcendentals=0),
         name="observe",
     )(read)
-    from_far = lax.ppermute(own, "tile", far)
-    from_near = lax.ppermute(own, "tile", near)
+    from_near, from_far = exchange(own, own)
     ens, mean, high, low = pl.pallas_call(
         own_kernel,
         out_shape=(

time: 72.1 us -> 71.6 us (level)
  no operation moved by 1% of the time
where the time goes in v3:
time: 71.6 us; the launch traced here: 71.3 us
  blocking collectives  34.2 us (48%)
  starting transfers between devices  27.1 us (38%)
  Pallas kernels  7.89 us (11%)
  waiting for transfers between devices  2 us (3%)
    ppermute x2, starting transfers between devices, exchange(): from_far = lax.ppermute(far_values, 'tile', far)  23.3 us
    all_to_all x1, blocking collectives, local(): lax.all_to_all(forecast.reshape(16, 32, 128), 'member', split_axis=0, con...  20 us
    all_to_all x1, blocking collectives, local(): lax.all_to_all(analysed.reshape(16, 32, 128), 'member', split_axis=0, con...  14.3 us
    ppermute x2, starting transfers between devices, exchange(): from_near = lax.ppermute(near_values, 'tile', near)  3.84 us
    pallas_call x1, Pallas kernels, local(): pl.pallas_call(forecast_kernel, out_shape=shape(512), in_specs=[VMEM] * 6...  2.79 us
    pallas_call x1, Pallas kernels, local(): pl.pallas_call(analysis_kernel, out_shape=shape(512), in_specs=[VMEM] * 1...  2.27 us
    ppermute x2, waiting for transfers between devices, exchange(): from_far = lax.ppermute(far_values, 'tile', far)  2 us
  transfers between devices with their start and end apart: 4, of which 2 were waited for; matrix products, arithmetic and copies ran while one was open for 0% of the time, Pallas kernels for 1%

profile of v3, /device:TPU:2, one launch (start us, length us, event | category | flops | bytes accessed | tf_op | source)
XLA Modules:
  0.0 71.3 jit_solution(15019695416641623708)
XLA Ops:
  0.0 1.0 %edges.1 = (bf16[96,128]{1,0:T(8,128)(2,1)S(1)}, bf16[96,128]{1,0:T(8,128)(2,1)S(1)}, bf16[512,128]{1,0:T(8,128)(2,1)S(1)}, bf16[9,4,32]{2,1,0:T(4,128)(2,1)S(1)...) custom-call(bf16[512,128]{1,0:T(8,128)(2,1)} %bitcast.27, ...), custom_call_target="tpu_custom_call" | custom-call | tf_op jit(solution)/shard_map/edges/pallas_call | solution.py:306
  1.1 1.9 %collective-permute-start = (bf16[96,128]{1,0:T(8,128)(2,1)S(1)}, bf16[96,128]{1,0:T(8,128)(2,1)S(1)}, u32[]{:S(2)}, u32[]{:S(2)}) collective-permute-start(bf16[96,128]{1,0:T(8,128)(2,1)S(1)} %get-tuple-element.23), channel_id=1, source_target_pairs={{0,1},{1,0},{2,3},{3,2},{4,5},{5,4},{6,7},{7,6},{8,9},{9,8},{10,11... | collective-permute-start | bytes 73736 | tf_op jit(solution)/shard_map/ppermute | solution.py:282
  3.0 18.3 %collective-permute-start.1 = (bf16[96,128]{1,0:T(8,128)(2,1)S(1)}, bf16[96,128]{1,0:T(8,128)(2,1)S(1)}, u32[]{:S(2)}, u32[]{:S(2)}) collective-permute-start(bf16[96,128]{1,0:T(8,128)(2,1)S(1)} %get-tuple-element.24), channel_id=1, source_target_pairs={{0,63},{1,2},{2,1},{3,4},{4,3},{5,6},{6,5},{7,8},{8,7},{9,10},{10,... | collective-permute-start | bytes 73736 | tf_op jit(solution)/shard_map/ppermute | solution.py:281
  21.3 0.4 weights.1
  21.7 0.0 collective-permute-done.near_ref
  21.8 1.0 %collective-permute-done.1.far_ref = bf16[96,128]{1,0:T(8,128)(2,1)S(1)} collective-permute-done((bf16[96,128]{1,0:T(8,128)(2,1)S(1)}, bf16[96,128]{1,0:T(8,128)(2,1)S(1)}, u32[]{:S(2)}, u32[]{:S(2)}) %collective-permute-start.1) | collective-permute-done | bytes 24608 | tf_op jit(solution)/shard_map/ppermute | solution.py:281
  22.8 2.8 %forecast.1 = bf16[512,128]{1,0:T(8,128)(2,1)S(1)} custom-call(bf16[512,128]{1,0:T(8,128)(2,1)S(1)} %get-tuple-element.22.state_ref, bf16[96,128]{1,0:T(8,128)(2,1)S(1)} %collective-permute-done.near_ref, bf16[96,128]{1,0:T(8,128)(2,1)S(1)} %collective-permute-done.1.far_ref, bf16[320,192]{1,0:T(8,128)(2,1)S(1)} %get-tuple-element.28.t1_ref, ...), custom_call_target="tpu_custom_call" | custom-call | tf_op jit(solution)/shard_map/forecast/pallas_call | solution.py:326
  25.6 20.0 %all_to_all.10 = bf16[16,32,128]{2,1,0:T(8,128)(2,1)S(1)} all-to-all(bf16[16,32,128]{2,1,0:T(8,128)(2,1)S(1)} %bitcast.26), channel_id=1, replica_groups=mesh['member'=16,'tile'=64] {'member'}, dimensions={0} | all-to-all | bytes 262144 | tf_op jit(solution)/shard_map/all_to_all | solution.py:341
  45.6 5.0 %collective-permute-start.3 = (bf16[512,128]{1,0:T(8,128)(2,1)S(1)}, bf16[512,128]{1,0:T(8,128)(2,1)S(1)}, u32[]{:S(2)}, u32[]{:S(2)}) collective-permute-start(bf16[512,128]{1,0:T(8,128)(2,1)S(1)} %bitcast.23), channel_id=1, source_target_pairs={{0,63},{1,2},{2,1},{3,4},{4,3},{5,6},{6,5},{7,8},{8,7},{9,10},{10,... | collective-permute-start | bytes 393224 | tf_op jit(solution)/shard_map/ppermute | solution.py:281
  50.5 1.9 %collective-permute-start.2 = (bf16[512,128]{1,0:T(8,128)(2,1)S(1)}, bf16[512,128]{1,0:T(8,128)(2,1)S(1)}, u32[]{:S(2)}, u32[]{:S(2)}) collective-permute-start(bf16[512,128]{1,0:T(8,128)(2,1)S(1)} %bitcast.24), channel_id=1, source_target_pairs={{0,1},{1,0},{2,3},{3,2},{4,5},{5,4},{6,7},{7,6},{8,9},{9,8},{10,11... | collective-permute-start | bytes 393224 | tf_op jit(solution)/shard_map/ppermute | solution.py:282
  52.5 0.3 observe.1.hot_ref
  52.7 0.3 own.1
  53.0 1.0 %collective-permute-done.3.far_ref = bf16[512,128]{1,0:T(8,128)(2,1)S(1)} collective-permute-done((bf16[512,128]{1,0:T(8,128)(2,1)S(1)}, bf16[512,128]{1,0:T(8,128)(2,1)S(1)}, u32[]{:S(2)}, u32[]{:S(2)}) %collective-permute-start.3) | collective-permute-done | bytes 131104 | tf_op jit(solution)/shard_map/ppermute | solution.py:281
  54.0 0.0 collective-permute-done.2.near_ref
  54.0 2.3 %analysis.1 = bf16[512,128]{1,0:T(8,128)(2,1)S(1)} custom-call(bf16[512,128]{1,0:T(8,128)(2,1)S(1)} %collective-permute-done.2.near_ref, bf16[512,128]{1,0:T(8,128)(2,1)S(1)} %collective-permute-done.3.far_ref, bf16[1536,512]{1,0:T(8,128)(2,1)S(1)} %observe.1.hot_ref, f32[128,512]{1,0:T(8,128)S(1)} %get-tuple-element.32.ens_ref, ...), custom_call_target="tpu_custom_call" | custom-call | tf_op jit(solution)/shard_map/analysis/pallas_call | solution.py:368
  56.2 14.3 %all_to_all.11 = bf16[16,32,128]{2,1,0:T(8,128)(2,1)S(1)} all-to-all(bf16[16,32,128]{2,1,0:T(8,128)(2,1)S(1)} %bitcast.21), channel_id=1, replica_groups=mesh['member'=16,'tile'=64] {'member'}, dimensions={0} | all-to-all | bytes 262144 | tf_op jit(solution)/shard_map/all_to_all | solution.py:377
  70.5 0.8 %unpack.1 = bf16[512,128]{1,0:T(8,128)(2,1)} custom-call(bf16[512,128]{1,0:T(8,128)(2,1)S(1)} %bitcast.22), custom_call_target="tpu_custom_call" | custom-call | tf_op jit(solution)/shard_map/unpack/pallas_call | solution.py:380
Async XLA Ops:
  1.1 20.7 %collective-permute-start = (bf16[96,128]{1,0:T(8,128)(2,1)S(1)}, bf16[96,128]{1,0:T(8,128)(2,1)S(1)}, u32[]{:S(2)}, u32[]{:S(2)}) collective-permute-start(bf16[96,128]{1,0:T(8,128)(2,1)S(1)} %get-tuple-element.23), channel_id=1, source_target_pairs={{0,1},{1,0},{2,3},{3,2},{4,5},{5,4},{6,7},{7,6},{8,9},{9,8},{10,11... | collective-permute-start | bytes 73736 | tf_op jit(solution)/shard_map/ppermute | solution.py:282
  3.0 19.8 %collective-permute-start.1 = (bf16[96,128]{1,0:T(8,128)(2,1)S(1)}, bf16[96,128]{1,0:T(8,128)(2,1)S(1)}, u32[]{:S(2)}, u32[]{:S(2)}) collective-permute-start(bf16[96,128]{1,0:T(8,128)(2,1)S(1)} %get-tuple-element.24), channel_id=1, source_target_pairs={{0,63},{1,2},{2,1},{3,4},{4,3},{5,6},{6,5},{7,8},{8,7},{9,10},{10,... | collective-permute-start | bytes 73736 | tf_op jit(solution)/shard_map/ppermute | solution.py:281
  45.6 8.4 %collective-permute-start.3 = (bf16[512,128]{1,0:T(8,128)(2,1)S(1)}, bf16[512,128]{1,0:T(8,128)(2,1)S(1)}, u32[]{:S(2)}, u32[]{:S(2)}) collective-permute-start(bf16[512,128]{1,0:T(8,128)(2,1)S(1)} %bitcast.23), channel_id=1, source_target_pairs={{0,63},{1,2},{2,1},{3,4},{4,3},{5,6},{6,5},{7,8},{8,7},{9,10},{10,... | collective-permute-start | bytes 393224 | tf_op jit(solution)/shard_map/ppermute | solution.py:281
  50.5 3.4 %collective-permute-start.2 = (bf16[512,128]{1,0:T(8,128)(2,1)S(1)}, bf16[512,128]{1,0:T(8,128)(2,1)S(1)}, u32[]{:S(2)}, u32[]{:S(2)}) collective-permute-start(bf16[512,128]{1,0:T(8,128)(2,1)S(1)} %bitcast.24), channel_id=1, source_target_pairs={{0,1},{1,0},{2,3},{3,2},{4,5},{5,4},{6,7},{7,6},{8,9},{9,8},{10,11... | collective-permute-start | bytes 393224 | tf_op jit(solution)/shard_map/ppermute | solution.py:282

commit v4 on v3

--- a/solution.py
+++ b/solution.py
@@ -9,6 +9,7 @@
 F32 = jnp.float32
 BF16 = jnp.bfloat16
 VMEM = pl.BlockSpec(memory_space=pltpu.VMEM)
+HBM = pl.BlockSpec(memory_space=pltpu.HBM)
 
 
 def params(mib):
@@ -31,22 +32,40 @@
     return out
 
 
+CUTS = 4
+CUT = 512 // CUTS
+
+
+def cut_copies(source, target, semaphores):
+    return [
+        pltpu.make_async_copy(
+            source.at[cut * CUT : (cut + 1) * CUT, :],
+            target.at[cut * CUT : (cut + 1) * CUT, :],
+            semaphores.at[cut],
+        )
+        for cut in range(CUTS)
+    ]
+
+
 def edges_kernel(*refs):
-    sources, (near_ref, far_ref), targets, (wide, arrived) = refs[:8], refs[8:10], refs[10:18], refs[18:]
+    (state_ref, *small), (near_ref, far_ref, wide) = refs[:8], refs[8:11]
+    targets, (rows, arrived) = refs[11:18], refs[18:]
     odd = lax.axis_index("tile") % 2
-    copies = [
-        pltpu.make_async_copy(source, target, arrived.at[number])
-        for number, (source, target) in enumerate(zip(sources, targets))
+    loads = cut_copies(state_ref, rows, arrived)
+    others = [
+        pltpu.make_async_copy(source, target, arrived.at[CUTS + number])
+        for number, (source, target) in enumerate(zip(small, targets))
     ]
-    for copy in copies:
+    for copy in loads + others:
         copy.start()
-    copies[0].wait()
-    wide[...] = targets[0][...].astype(F32)
+    for cut, copy in enumerate(loads):
+        copy.wait()
+        wide[cut * CUT : (cut + 1) * CUT, :] = rows[cut * CUT : (cut + 1) * CUT, :].astype(F32)
     for row in range(3):
         place = slice(row * 32, (row + 1) * 32)
         near_ref[place, :] = wide[pl.ds(13 * (1 - odd) + row, 32, stride=16), :].astype(BF16)
         far_ref[place, :] = wide[pl.ds(13 * odd + row, 32, stride=16), :].astype(BF16)
-    for copy in copies[1:]:
+    for copy in others:
         copy.wait()
 
 
@@ -56,7 +75,7 @@
         ref[start : start + 16, :] = value[block * 16 : block * 16 + 16]
 
 
-def weights_kernel(first_ref, middle_ref, last_ref, t1_ref, t2_ref, t3_ref):
+def weights_kernel(first_ref, middle_ref, last_ref, inner_ref, outer_ref, t2_ref, t3_ref):
     where_to = iota((4, 192), 1) // 16
     expanded = []
     for dy in range(3):
@@ -67,8 +86,10 @@
                 first_ref[dy * 3 + dx], spread, (((0,), (0,)), ((), ())), preferred_element_type=F32
             )
         expanded.append(jnp.concatenate([total] * 10, axis=0))
-    distance = iota((320, 192), 1) % 16 - iota((320, 192), 0) // 32
-    t1_ref[...] = pick(distance, expanded).astype(BF16)
+    row = iota((320, 192), 0) // 32
+    distance = iota((320, 192), 1) % 16 - row
+    inner_ref[...] = pick(distance - 2, expanded).astype(BF16)
+    outer_ref[...] = pick(distance - jnp.where(row >= 5, 3, 0), expanded).astype(BF16)
     distance = iota((192, 256), 1) // 32 - iota((192, 256), 0) // 32
     for dx in range(3):
         taps = []
@@ -90,25 +111,35 @@
         spread_blocks(t3_ref, dx, pick(distance, taps).astype(BF16)[:, :576])
 
 
+def first_layer(rows, weights, pair):
+    sides = []
+    for member in (2 * pair, 2 * pair + 1):
+        own = rows[member * 64 : (member + 1) * 64, :]
+        sides.append(jnp.concatenate([pltpu.roll(own, 1, 1), own, pltpu.roll(own, 127, 1)], axis=0))
+    columns = jnp.concatenate(sides, axis=1).astype(BF16)
+    return jnp.dot(weights[...], columns, preferred_element_type=F32)
+
+
+def inner_kernel(wide, weights_ref, inside_ref):
+    for pair in range(4):
+        inside_ref[pair] = silu(first_layer(wide, weights_ref, pair)).astype(BF16)
+
+
 def forecast_kernel(
-    state_ref, near_ref, far_ref, t1_ref, t2_ref, t3_ref, out_ref, wide, padded, h1, h2, sent
+    wide, near_ref, far_ref, outer_ref, t2_ref, t3_ref, inside, out_ref, edge, outside, h2, sent
 ):
     odd = lax.axis_index("tile") % 2
-    wide[...] = state_ref[...].astype(F32)
-    nothing = jnp.zeros((32, 128), F32)
     for row in range(16):
-        if 3 <= row < 12:
-            padded[pl.ds(row, 32, stride=16), :] = wide[pl.ds(row - 3, 32, stride=16), :]
-        if row < 9:
-            padded[pl.ds(512 + row, 32, stride=16), :] = wide[pl.ds(row + 7, 32, stride=16), :]
-        if row >= 12:
-            padded[pl.ds(row, 32, stride=16), :] = nothing
-            padded[pl.ds(512 + row, 32, stride=16), :] = nothing
+        if row % 8 == 7:
+            edge[pl.ds(row, 32, stride=16), :] = jnp.zeros((32, 128), F32)
+        elif 3 <= row < 12:
+            own = row - 3 if row < 7 else row + 4
+            edge[pl.ds(row, 32, stride=16), :] = wide[pl.ds(own, 32, stride=16), :]
     for row in range(3):
         place = slice(row * 32, (row + 1) * 32)
-        near_at, far_at = 521 * (1 - odd) + row, 521 * odd + row
-        padded[pl.ds(near_at, 32, stride=16), :] = near_ref[place, :].astype(F32)
-        padded[pl.ds(far_at, 32, stride=16), :] = far_ref[place, :].astype(F32)
+        near_at, far_at = 12 * (1 - odd) + row, 12 * odd + row
+        edge[pl.ds(near_at, 32, stride=16), :] = near_ref[place, :].astype(F32)
+        edge[pl.ds(far_at, 32, stride=16), :] = far_ref[place, :].astype(F32)
 
     def lanes(side):
         return slice(side * 128, (side + 1) * 128)
@@ -118,21 +149,18 @@
         left, middle, right = (part[:, dx].reshape(rows, 128) for dx in range(3))
         return middle + pltpu.roll(left, 1, 1) + pltpu.roll(right, 127, 1)
 
-    def first(pair, half):
-        sides = []
-        for member in (2 * pair, 2 * pair + 1):
-            start = half * 512 + member * 64
-            rows = padded[start : start + 64, :]
-            sides.append(
-                jnp.concatenate([pltpu.roll(rows, 1, 1), rows, pltpu.roll(rows, 127, 1)], axis=0)
-            )
-        columns = jnp.concatenate(sides, axis=1).astype(BF16)
-        summed = jnp.dot(t1_ref[...], columns, preferred_element_type=F32)
+    def first(pair):
+        summed = first_layer(edge, outer_ref, pair)
         yield
-        h1[pair, half * 320 : (half + 1) * 320, :] = silu(summed).astype(BF16)
+        outside[pair] = silu(summed).astype(BF16)
 
     def second(pair, group):
-        columns = h1[pair, group * 192 : group * 192 + 256, :]
+        if group == 0:
+            columns = jnp.concatenate([outside[pair, :160, :], inside[pair, :96, :]], axis=0)
+        elif group == 1:
+            columns = inside[pair, 32:288, :]
+        else:
+            columns = jnp.concatenate([inside[pair, 224:, :], outside[pair, 160:, :]], axis=0)
         taps = jnp.dot(t2_ref[...], columns, preferred_element_type=F32)
         yield
         for side in range(2):
@@ -150,10 +178,10 @@
                 sent[pl.ds(f * 8 + member, 16, stride=32), :] = result[f * 16 : (f + 1) * 16]
 
     order = []
-    for pairs in ((0, 1, 2, 3),):
-        order += [first(pair, half) for half in range(2) for pair in pairs]
-        order += [second(pair, group) for group in range(3) for pair in pairs]
-        order += [third(pair) for pair in pairs]
+    for pair in range(4):
+        order += [second(pair, 1), first(pair)]
+    order += [second(pair, group) for group in (0, 2) for pair in range(4)]
+    order += [third(pair) for pair in range(4)]
     pending = []
     for task in order:
         next(task)
@@ -170,13 +198,14 @@
     return high, (value - high.astype(F32)).astype(BF16)
 
 
+def plain_dot(left, right, contract):
+    return lax.dot_general(left, right, (contract, ((), ())), preferred_element_type=F32)
+
+
 def fine_dot(a, b, contract=((1,), (0,))):
     (a_high, a_low), (b_high, b_low) = a, b
-
-    def one(left, right):
-        return lax.dot_general(left, right, (contract, ((), ())), preferred_element_type=F32)
-
-    return one(a_high, b_high) + (one(a_high, b_low) + one(a_low, b_high))
+    rest = plain_dot(a_high, b_low, contract) + plain_dot(a_low, b_high, contract)
+    return plain_dot(a_high, b_high, contract) + rest
 
 
 def members_by_points(ref):
@@ -231,39 +260,53 @@
     anom = obs_ens - obs_mean
     weight = jnp.exp(-0.25 * class_ref[...].astype(F32)) / var_ref[...]
     identity = (iota((size, size), 0) == iota((size, size), 1)).astype(F32)
-    gram = (size - 1.0) * identity + fine_dot(split(anom), split(anom * weight), ((1,), (1,)))
+    high, low = split(anom)
+    both = jnp.concatenate(split(anom * weight), axis=0)
+    wide = plain_dot(high, both, ((1,), (1,)))
+    gram = (size - 1.0) * identity + wide[:, :size]
+    gram += wide[:, size:] + plain_dot(low, both[:size], ((1,), (1,)))
     residual = jnp.sum(anom * (weight * (obs_ref[...] - obs_mean)), axis=1, keepdims=True)
-    square = jnp.sum(jnp.sum(gram * gram, axis=1, keepdims=True), axis=0, keepdims=True)
-    norm = jnp.sqrt(square)
-    y = gram * (1.0 / norm)
+    parts = split(gram)
+    square = fine_dot(parts, parts)
+    total = jnp.sum(jnp.sum(gram * gram, axis=0, keepdims=True), axis=1, keepdims=True)
+    norm = jnp.sqrt(total)
+    scale = 1.0 / norm
+    y = gram * scale
     z = 1.5 * identity - 0.5 * y
-    y_parts, z_parts = split(y), split(z)
-    y_parts = split(fine_dot(y_parts, z_parts))
+    y_parts, z_parts = split(1.5 * y - 0.5 * ((square * scale) * scale)), split(z)
     for sweep in range(1, NS_ITERS):
-        factor = split(1.5 * identity - 0.5 * fine_dot(z_parts, y_parts))
+        factor = 1.5 * identity - 0.5 * fine_dot(z_parts, y_parts)
+        factor_parts = split(factor)
         if sweep + 1 < NS_ITERS:
-            y_parts = split(fine_dot(y_parts, factor))
-        z = fine_dot(factor, z_parts)
-        z_parts = split(z)
-    root = z * (1.0 / jnp.sqrt(norm))
-    once = jnp.sum(root * residual, axis=0, keepdims=True)
-    mean_weights = jnp.sum(root * once, axis=1, keepdims=True)
+            y_parts = split(fine_dot(y_parts, factor_parts))
+            z = fine_dot(factor_parts, z_parts)
+            z_parts = split(z)
+    across = jnp.sum(z * residual, axis=0, keepdims=True)
+    twice = jnp.sum(z * across, axis=1, keepdims=True) * scale
+    across = jnp.sum(factor * twice, axis=0, keepdims=True)
+    mean_weights = jnp.sum(factor * across, axis=1, keepdims=True)
+    root = fine_dot(factor_parts, z_parts) * (((size - 1.0) ** 0.5) / jnp.sqrt(norm))
     high, low = high_ref[...], low_ref[...]
     anomaly = high.astype(F32) + low.astype(F32)
     shift = shift_ref[...] + jnp.sum(mean_weights * anomaly, axis=0, keepdims=True)
-    result = shift + fine_dot(split(root * (size - 1.0) ** 0.5), (high, low))
+    result = shift + fine_dot(split(root), (high, low))
     for f in range(4):
         held[:, f] = result[:, f * 128 : (f + 1) * 128].reshape(16, 8, 128)
     out_ref[...] = held[...].reshape(512, 128).astype(BF16)
 
 
-def unpack_kernel(in_ref, out_ref, wide):
+def unpack_kernel(in_ref, out_ref, wide, rows, stored):
     wide[...] = in_ref[...].astype(F32)
+    stores = cut_copies(rows, out_ref, stored)
     for lane in range(32):
         member, f = lane // 4, lane % 4
-        out_ref[lane * 16 : (lane + 1) * 16, :] = wide[
+        rows[lane * 16 : (lane + 1) * 16, :] = wide[
             pl.ds(f * 8 + member, 16, stride=32), :
         ].astype(BF16)
+        if (lane + 1) * 16 % CUT == 0:
+            stores[lane * 16 // CUT].start()
+    for copy in stores:
+        copy.wait()
 
 
 def shape(rows, columns=128):
@@ -303,41 +346,51 @@
         observation_rows.reshape(1, 512),
         loc_class.reshape(1, 512),
     )
-    near_edge, far_edge, rows, first, middle, last, obs, variance, read, classes = pl.pallas_call(
+    near_edge, far_edge, wide, first, middle, last, obs, variance, read, classes = pl.pallas_call(
         edges_kernel,
-        out_shape=(shape(96), shape(96))
-        + tuple(jax.ShapeDtypeStruct(a.shape, a.dtype) for a in given),
-        in_specs=[pl.BlockSpec(memory_space=pltpu.HBM)] * 8,
+        out_shape=(shape(96), shape(96), jax.ShapeDtypeStruct((512, 128), F32))
+        + tuple(jax.ShapeDtypeStruct(a.shape, a.dtype) for a in given[1:]),
+        in_specs=[HBM] * 8,
         out_specs=(VMEM,) * 10,
-        scratch_shapes=[scratch(512, 128), pltpu.SemaphoreType.DMA((8,))],
+        scratch_shapes=[scratch(512, 128, dtype=BF16), pltpu.SemaphoreType.DMA((CUTS + 7,))],
         compiler_params=params(8),
         name="edges",
     )(*(pltpu.with_memory_space_constraint(a, pltpu.HBM) for a in given))
     from_near, from_far = exchange(near_edge, far_edge)
-    t1, t2, t3 = pl.pallas_call(
+    inner, outer, t2, t3 = pl.pallas_call(
         weights_kernel,
-        out_shape=(shape(320, 192), shape(576, 256), shape(192, 576)),
+        out_shape=(shape(320, 192), shape(320, 192), shape(576, 256), shape(192, 576)),
         in_specs=[VMEM] * 3,
-        out_specs=(VMEM,) * 3,
+        out_specs=(VMEM,) * 4,
         compiler_params=params(8),
         cost_estimate=pl.CostEstimate(flops=4000000, bytes_accessed=700000, transcendentals=0),
         name="weights",
     )(first, middle, last)
+    inside = pl.pallas_call(
+        inner_kernel,
+        out_shape=jax.ShapeDtypeStruct((4, 320, 256), BF16),
+        in_specs=[VMEM] * 2,
+        out_specs=VMEM,
+        compiler_params=params(8),
+        cost_estimate=pl.CostEstimate(
+            flops=130000000, bytes_accessed=1000000, transcendentals=330000
+        ),
+        name="inner",
+    )(wide, inner)
     forecast = pl.pallas_call(
         forecast_kernel,
         out_shape=shape(512),
-        in_specs=[VMEM] * 6,
+        in_specs=[VMEM] * 7,
         out_specs=VMEM,
         scratch_shapes=[
             scratch(512, 128),
-            scratch(1024, 128),
-            scratch(4, 640, 256, dtype=BF16),
+            scratch(4, 320, 256, dtype=BF16),
             scratch(4, 576, 256, dtype=BF16),
             scratch(512, 128),
         ],
         compiler_params=params(16),
         name="forecast",
-    )(rows, from_near, from_far, t1, t2, t3)
+    )(wide, from_near, from_far, outer, t2, t3, inside)
     own = lax.all_to_all(
         forecast.reshape(16, 32, 128), "member", split_axis=0, concat_axis=0, tiled=True
     ).reshape(512, 128)
@@ -381,8 +434,12 @@
         unpack_kernel,
         out_shape=shape(512),
         in_specs=[VMEM],
-        out_specs=VMEM,
-        scratch_shapes=[scratch(512, 128)],
+        out_specs=HBM,
+        scratch_shapes=[
+            scratch(512, 128),
+            scratch(512, 128, dtype=BF16),
+            pltpu.SemaphoreType.DMA((CUTS,)),
+        ],
         compiler_params=params(8),
         name="unpack",
     )(returned)

time: 71.6 us -> 70.9 us (level)
    pallas_call x3 -> x4, Pallas kernels: 4.28 us -> 4.39 us  [the longest x1 2.2 us: local(): pl.pallas_call(forecast_kernel, out_shape=shape(512), in_specs=[VMEM] * 7...]
  transfers between devices with their start and end apart: 4 -> 4, of which waited for: 2 -> 2; matrix products, arithmetic and copies ran while one was open for 0% -> 0% of each run, Pallas kernels for 1% -> 2%
where the time goes in v4:
time: 70.9 us; the launch traced here: 70.6 us
  blocking collectives  34.3 us (48%)
  starting transfers between devices  27.1 us (38%)
  Pallas kernels  7.77 us (11%)
  waiting for transfers between devices  1.33 us (2%)
    ppermute x2, starting transfers between devices, exchange(): from_far = lax.ppermute(far_values, 'tile', far)  23.3 us
    all_to_all x1, blocking collectives, local(): lax.all_to_all(forecast.reshape(16, 32, 128), 'member', split_axis=0, con...  20 us
    all_to_all x1, blocking collectives, local(): lax.all_to_all(analysed.reshape(16, 32, 128), 'member', split_axis=0, con...  14.3 us
    ppermute x2, starting transfers between devices, exchange(): from_near = lax.ppermute(near_values, 'tile', near)  3.84 us
    pallas_call x1, Pallas kernels, local(): pl.pallas_call(forecast_kernel, out_shape=shape(512), in_specs=[VMEM] * 7...  2.2 us
    pallas_call x1, Pallas kernels, local(): pl.pallas_call(analysis_kernel, out_shape=shape(512), in_specs=[VMEM] * 1...  2.06 us
  transfers between devices with their start and end apart: 4, of which 2 were waited for; matrix products, arithmetic and copies ran while one was open for 0% of the time, Pallas kernels for 2%

profile of v4, /device:TPU:2, one launch (start us, length us, event | category | flops | bytes accessed | tf_op | source)
XLA Modules:
  0.0 70.6 jit_solution(10613050659857140960)
XLA Ops:
  0.0 1.1 %edges.1 = (bf16[96,128]{1,0:T(8,128)(2,1)S(1)}, bf16[96,128]{1,0:T(8,128)(2,1)S(1)}, f32[512,128]{1,0:T(8,128)S(1)}, bf16[9,4,32]{2,1,0:T(4,128)(2,1)S(1)}, bf1...) custom-call(bf16[512,128]{1,0:T(8,128)(2,1)} %bitcast.27, ...), custom_call_target="tpu_custom_call" | custom-call | tf_op jit(solution)/shard_map/edges/pallas_call | solution.py:349
  1.1 1.9 %collective-permute-start = (bf16[96,128]{1,0:T(8,128)(2,1)S(1)}, bf16[96,128]{1,0:T(8,128)(2,1)S(1)}, u32[]{:S(2)}, u32[]{:S(2)}) collective-permute-start(bf16[96,128]{1,0:T(8,128)(2,1)S(1)} %get-tuple-element.24), channel_id=1, source_target_pairs={{0,1},{1,0},{2,3},{3,2},{4,5},{5,4},{6,7},{7,6},{8,9},{9,8},{10,11... | collective-permute-start | bytes 73736 | tf_op jit(solution)/shard_map/ppermute | solution.py:325
  3.0 18.3 %collective-permute-start.1 = (bf16[96,128]{1,0:T(8,128)(2,1)S(1)}, bf16[96,128]{1,0:T(8,128)(2,1)S(1)}, u32[]{:S(2)}, u32[]{:S(2)}) collective-permute-start(bf16[96,128]{1,0:T(8,128)(2,1)S(1)} %get-tuple-element.25), channel_id=1, source_target_pairs={{0,63},{1,2},{2,1},{3,4},{4,3},{5,6},{6,5},{7,8},{8,7},{9,10},{10,... | collective-permute-start | bytes 73736 | tf_op jit(solution)/shard_map/ppermute | solution.py:324
  21.3 0.6 weights.1
  22.0 0.5 inner.1.inside
  22.4 0.0 collective-permute-done.near_ref
  22.5 0.4 collective-permute-done.1.far_ref
  22.8 2.2 %forecast.1 = bf16[512,128]{1,0:T(8,128)(2,1)S(1)} custom-call(f32[512,128]{1,0:T(8,128)S(1)} %get-tuple-element.23.wide, bf16[96,128]{1,0:T(8,128)(2,1)S(1)} %collective-permute-done.near_ref, bf16[96,128]{1,0:T(8,128)(2,1)S(1)} %collective-permute-done.1.far_ref, bf16[320,192]{1,0:T(8,128)(2,1)S(1)} %get-tuple-element.29.outer_ref, ...), custom_call_target="tpu_custom_call" | custom-call | tf_op jit(solution)/shard_map/forecast/pallas_call | solution.py:380
  25.0 20.0 %all_to_all.10 = bf16[16,32,128]{2,1,0:T(8,128)(2,1)S(1)} all-to-all(bf16[16,32,128]{2,1,0:T(8,128)(2,1)S(1)} %bitcast.22), channel_id=1, replica_groups=mesh['member'=16,'tile'=64] {'member'}, dimensions={0} | all-to-all | bytes 262144 | tf_op jit(solution)/shard_map/all_to_all | solution.py:394
  45.0 5.0 %collective-permute-start.3 = (bf16[512,128]{1,0:T(8,128)(2,1)S(1)}, bf16[512,128]{1,0:T(8,128)(2,1)S(1)}, u32[]{:S(2)}, u32[]{:S(2)}) collective-permute-start(bf16[512,128]{1,0:T(8,128)(2,1)S(1)} %bitcast.24), channel_id=1, source_target_pairs={{0,63},{1,2},{2,1},{3,4},{4,3},{5,6},{6,5},{7,8},{8,7},{9,10},{10,... | collective-permute-start | bytes 393224 | tf_op jit(solution)/shard_map/ppermute | solution.py:324
  50.0 1.9 %collective-permute-start.2 = (bf16[512,128]{1,0:T(8,128)(2,1)S(1)}, bf16[512,128]{1,0:T(8,128)(2,1)S(1)}, u32[]{:S(2)}, u32[]{:S(2)}) collective-permute-start(bf16[512,128]{1,0:T(8,128)(2,1)S(1)} %bitcast.25), channel_id=1, source_target_pairs={{0,1},{1,0},{2,3},{3,2},{4,5},{5,4},{6,7},{7,6},{8,9},{9,8},{10,11... | collective-permute-start | bytes 393224 | tf_op jit(solution)/shard_map/ppermute | solution.py:325
  51.9 0.3 observe.1.hot_ref
  52.2 0.2 own.1
  52.4 1.0 %collective-permute-done.3.far_ref = bf16[512,128]{1,0:T(8,128)(2,1)S(1)} collective-permute-done((bf16[512,128]{1,0:T(8,128)(2,1)S(1)}, bf16[512,128]{1,0:T(8,128)(2,1)S(1)}, u32[]{:S(2)}, u32[]{:S(2)}) %collective-permute-start.3) | collective-permute-done | bytes 131104 | tf_op jit(solution)/shard_map/ppermute | solution.py:324
  53.4 0.0 collective-permute-done.2.near_ref
  53.4 2.1 %analysis.1 = bf16[512,128]{1,0:T(8,128)(2,1)S(1)} custom-call(bf16[512,128]{1,0:T(8,128)(2,1)S(1)} %collective-permute-done.2.near_ref, bf16[512,128]{1,0:T(8,128)(2,1)S(1)} %collective-permute-done.3.far_ref, bf16[1536,512]{1,0:T(8,128)(2,1)S(1)} %observe.1.hot_ref, f32[128,512]{1,0:T(8,128)S(1)} %get-tuple-element.34.ens_ref, ...), custom_call_target="tpu_custom_call" | custom-call | tf_op jit(solution)/shard_map/analysis/pallas_call | solution.py:421
  55.5 14.3 %all_to_all.11 = bf16[16,32,128]{2,1,0:T(8,128)(2,1)S(1)} all-to-all(bf16[16,32,128]{2,1,0:T(8,128)(2,1)S(1)} %bitcast.21), channel_id=1, replica_groups=mesh['member'=16,'tile'=64] {'member'}, dimensions={0} | all-to-all | bytes 262144 | tf_op jit(solution)/shard_map/all_to_all | solution.py:430
  69.7 0.8 %unpack.1 = bf16[512,128]{1,0:T(8,128)(2,1)} custom-call(bf16[512,128]{1,0:T(8,128)(2,1)S(1)} %bitcast.23), custom_call_target="tpu_custom_call" | custom-call | tf_op jit(solution)/shard_map/unpack/pallas_call | solution.py:433
Async XLA Ops:
  1.1 21.4 %collective-permute-start = (bf16[96,128]{1,0:T(8,128)(2,1)S(1)}, bf16[96,128]{1,0:T(8,128)(2,1)S(1)}, u32[]{:S(2)}, u32[]{:S(2)}) collective-permute-start(bf16[96,128]{1,0:T(8,128)(2,1)S(1)} %get-tuple-element.24), channel_id=1, source_target_pairs={{0,1},{1,0},{2,3},{3,2},{4,5},{5,4},{6,7},{7,6},{8,9},{9,8},{10,11... | collective-permute-start | bytes 73736 | tf_op jit(solution)/shard_map/ppermute | solution.py:325
  3.0 19.8 %collective-permute-start.1 = (bf16[96,128]{1,0:T(8,128)(2,1)S(1)}, bf16[96,128]{1,0:T(8,128)(2,1)S(1)}, u32[]{:S(2)}, u32[]{:S(2)}) collective-permute-start(bf16[96,128]{1,0:T(8,128)(2,1)S(1)} %get-tuple-element.25), channel_id=1, source_target_pairs={{0,63},{1,2},{2,1},{3,4},{4,3},{5,6},{6,5},{7,8},{8,7},{9,10},{10,... | collective-permute-start | bytes 73736 | tf_op jit(solution)/shard_map/ppermute | solution.py:324
  45.0 8.4 %collective-permute-start.3 = (bf16[512,128]{1,0:T(8,128)(2,1)S(1)}, bf16[512,128]{1,0:T(8,128)(2,1)S(1)}, u32[]{:S(2)}, u32[]{:S(2)}) collective-permute-start(bf16[512,128]{1,0:T(8,128)(2,1)S(1)} %bitcast.24), channel_id=1, source_target_pairs={{0,63},{1,2},{2,1},{3,4},{4,3},{5,6},{6,5},{7,8},{8,7},{9,10},{10,... | collective-permute-start | bytes 393224 | tf_op jit(solution)/shard_map/ppermute | solution.py:324
  50.0 3.4 %collective-permute-start.2 = (bf16[512,128]{1,0:T(8,128)(2,1)S(1)}, bf16[512,128]{1,0:T(8,128)(2,1)S(1)}, u32[]{:S(2)}, u32[]{:S(2)}) collective-permute-start(bf16[512,128]{1,0:T(8,128)(2,1)S(1)} %bitcast.25), channel_id=1, source_target_pairs={{0,1},{1,0},{2,3},{3,2},{4,5},{5,4},{6,7},{7,6},{8,9},{9,8},{10,11... | collective-permute-start | bytes 393224 | tf_op jit(solution)/shard_map/ppermute | solution.py:325

commit v5 on v4

--- a/solution.py
+++ b/solution.py
@@ -69,6 +69,10 @@
         copy.wait()
 
 
+def plain_dot(left, right, contract):
+    return lax.dot_general(left, right, (contract, ((), ())), preferred_element_type=F32)
+
+
 def spread_blocks(ref, dx, value):
     for block in range(value.shape[0] // 16):
         start = block * 48 + dx * 16
@@ -76,28 +80,38 @@
 
 
 def weights_kernel(first_ref, middle_ref, last_ref, inner_ref, outer_ref, t2_ref, t3_ref):
-    where_to = iota((4, 192), 1) // 16
-    expanded = []
+    spot = iota((32, 256), 1) % 16
+    base = jnp.zeros((32, 256), F32)
     for dy in range(3):
-        total = jnp.zeros((32, 192), F32)
         for dx in range(3):
-            spread = (where_to == iota((4, 192), 0) + 4 * dx).astype(BF16)
-            total += lax.dot_general(
-                first_ref[dy * 3 + dx], spread, (((0,), (0,)), ((), ())), preferred_element_type=F32
-            )
-        expanded.append(jnp.concatenate([total] * 10, axis=0))
-    row = iota((320, 192), 0) // 32
-    distance = iota((320, 192), 1) % 16 - row
-    inner_ref[...] = pick(distance - 2, expanded).astype(BF16)
-    outer_ref[...] = pick(distance - jnp.where(row >= 5, 3, 0), expanded).astype(BF16)
-    distance = iota((192, 256), 1) // 32 - iota((192, 256), 0) // 32
+            spread = (iota((4, 256), 1) // 16 == iota((4, 256), 0) + 4 * dx).astype(BF16)
+            tap = plain_dot(first_ref[dy * 3 + dx], spread, ((0,), (0,)))
+            base += jnp.where(spot == dy, tap, 0.0)
+    for shift in range(13):
+        block = pltpu.roll(base, shift, 1)[:, :192].astype(BF16)
+        if 2 <= shift < 12:
+            inner_ref[(shift - 2) * 32 : (shift - 1) * 32, :] = block
+        if shift < 5 or shift >= 8:
+            edge = shift if shift < 5 else shift - 3
+            outer_ref[edge * 32 : (edge + 1) * 32, :] = block
+    lane = iota((32, 128), 1)
+    nothing = jnp.zeros((32, 128), F32)
     for dx in range(3):
-        taps = []
-        for dy in range(3):
-            one = middle_ref[dy * 3 + dx].astype(F32)
-            wide = jnp.concatenate([one] * 8, axis=1)
-            taps.append(jnp.concatenate([wide] * 6, axis=0))
-        spread_blocks(t2_ref, dx, pick(distance, taps).astype(BF16))
+        parts = [middle_ref[dy * 3 + dx].astype(F32) for dy in range(3)]
+        base = jnp.concatenate(parts + [nothing[:, :32]], axis=1)
+        for row in range(6):
+            moved = pltpu.roll(base, 32 * (row % 4), 1) if row % 4 else base
+            if row < 2:
+                halves = (moved, nothing)
+            elif row < 4:
+                kept = lane >= 32 * row
+                halves = (jnp.where(kept, moved, 0.0), jnp.where(kept, 0.0, moved))
+            else:
+                halves = (nothing, moved)
+            block = jnp.concatenate(halves, axis=1).astype(BF16)
+            for half in range(2):
+                start = (row * 2 + half) * 48 + dx * 16
+                t2_ref[start : start + 16, :] = block[half * 16 : half * 16 + 16]
     distance = iota((64, 640), 1) // 32 - iota((64, 640), 0) % 16
     for dx in range(3):
         taps = []
@@ -198,14 +212,14 @@
     return high, (value - high.astype(F32)).astype(BF16)
 
 
-def plain_dot(left, right, contract):
-    return lax.dot_general(left, right, (contract, ((), ())), preferred_element_type=F32)
-
-
-def fine_dot(a, b, contract=((1,), (0,))):
+def fine_dot(a, b):
     (a_high, a_low), (b_high, b_low) = a, b
-    rest = plain_dot(a_high, b_low, contract) + plain_dot(a_low, b_high, contract)
-    return plain_dot(a_high, b_high, contract) + rest
+    both = plain_dot(
+        jnp.concatenate([a_high, a_low], axis=1),
+        jnp.concatenate([b_high, b_high], axis=0),
+        ((1,), (0,)),
+    )
+    return both + plain_dot(a_high, b_low, ((1,), (0,)))
 
 
 def members_by_points(ref):

time: 70.9 us -> 70.8 us (level)
  no operation moved by 1% of the time
where the time goes in v5:
time: 70.8 us; the launch traced here: 70.5 us
  blocking collectives  34.2 us (48%)
  starting transfers between devices  27.1 us (38%)
  Pallas kernels  7.43 us (10%)
  waiting for transfers between devices  1.62 us (2%)
    ppermute x2, starting transfers between devices, exchange(): from_far = lax.ppermute(far_values, 'tile', far)  23.3 us
    all_to_all x1, blocking collectives, local(): lax.all_to_all(forecast.reshape(16, 32, 128), 'member', split_axis=0, con...  20 us
    all_to_all x1, blocking collectives, local(): lax.all_to_all(analysed.reshape(16, 32, 128), 'member', split_axis=0, con...  14.3 us
    ppermute x2, starting transfers between devices, exchange(): from_near = lax.ppermute(near_values, 'tile', near)  3.84 us
    pallas_call x1, Pallas kernels, local(): pl.pallas_call(forecast_kernel, out_shape=shape(512), in_specs=[VMEM] * 7...  2.2 us
    pallas_call x1, Pallas kernels, local(): pl.pallas_call(analysis_kernel, out_shape=shape(512), in_specs=[VMEM] * 1...  2 us
    ppermute x2, waiting for transfers between devices, exchange(): from_far = lax.ppermute(far_values, 'tile', far)  1.62 us
  transfers between devices with their start and end apart: 4, of which 2 were waited for; matrix products, arithmetic and copies ran while one was open for 0% of the time, Pallas kernels for 2%

profile of v5, /device:TPU:2, one launch (start us, length us, event | category | flops | bytes accessed | tf_op | source)
XLA Modules:
  0.0 70.5 jit_solution(13973177235592282021)
XLA Ops:
  0.0 1.1 %edges.1 = (bf16[96,128]{1,0:T(8,128)(2,1)S(1)}, bf16[96,128]{1,0:T(8,128)(2,1)S(1)}, f32[512,128]{1,0:T(8,128)S(1)}, bf16[9,4,32]{2,1,0:T(4,128)(2,1)S(1)}, bf1...) custom-call(bf16[512,128]{1,0:T(8,128)(2,1)} %bitcast.27, ...), custom_call_target="tpu_custom_call" | custom-call | tf_op jit(solution)/shard_map/edges/pallas_call | solution.py:363
  1.1 1.9 %collective-permute-start = (bf16[96,128]{1,0:T(8,128)(2,1)S(1)}, bf16[96,128]{1,0:T(8,128)(2,1)S(1)}, u32[]{:S(2)}, u32[]{:S(2)}) collective-permute-start(bf16[96,128]{1,0:T(8,128)(2,1)S(1)} %get-tuple-element.24), channel_id=1, source_target_pairs={{0,1},{1,0},{2,3},{3,2},{4,5},{5,4},{6,7},{7,6},{8,9},{9,8},{10,11... | collective-permute-start | bytes 73736 | tf_op jit(solution)/shard_map/ppermute | solution.py:339
  3.0 18.3 %collective-permute-start.1 = (bf16[96,128]{1,0:T(8,128)(2,1)S(1)}, bf16[96,128]{1,0:T(8,128)(2,1)S(1)}, u32[]{:S(2)}, u32[]{:S(2)}) collective-permute-start(bf16[96,128]{1,0:T(8,128)(2,1)S(1)} %get-tuple-element.25), channel_id=1, source_target_pairs={{0,63},{1,2},{2,1},{3,4},{4,3},{5,6},{6,5},{7,8},{8,7},{9,10},{10,... | collective-permute-start | bytes 73736 | tf_op jit(solution)/shard_map/ppermute | solution.py:338
  21.3 0.3 weights.1
  21.7 0.5 inner.1.inside
  22.2 0.0 collective-permute-done.near_ref
  22.2 0.7 collective-permute-done.1.far_ref
  22.8 2.2 %forecast.1 = bf16[512,128]{1,0:T(8,128)(2,1)S(1)} custom-call(f32[512,128]{1,0:T(8,128)S(1)} %get-tuple-element.23.wide, bf16[96,128]{1,0:T(8,128)(2,1)S(1)} %collective-permute-done.near_ref, bf16[96,128]{1,0:T(8,128)(2,1)S(1)} %collective-permute-done.1.far_ref, bf16[320,192]{1,0:T(8,128)(2,1)S(1)} %get-tuple-element.29.outer_ref, ...), custom_call_target="tpu_custom_call" | custom-call | tf_op jit(solution)/shard_map/forecast/pallas_call | solution.py:394
  25.0 20.0 %all_to_all.10 = bf16[16,32,128]{2,1,0:T(8,128)(2,1)S(1)} all-to-all(bf16[16,32,128]{2,1,0:T(8,128)(2,1)S(1)} %bitcast.22), channel_id=1, replica_groups=mesh['member'=16,'tile'=64] {'member'}, dimensions={0} | all-to-all | bytes 262144 | tf_op jit(solution)/shard_map/all_to_all | solution.py:408
  45.0 5.0 %collective-permute-start.3 = (bf16[512,128]{1,0:T(8,128)(2,1)S(1)}, bf16[512,128]{1,0:T(8,128)(2,1)S(1)}, u32[]{:S(2)}, u32[]{:S(2)}) collective-permute-start(bf16[512,128]{1,0:T(8,128)(2,1)S(1)} %bitcast.24), channel_id=1, source_target_pairs={{0,63},{1,2},{2,1},{3,4},{4,3},{5,6},{6,5},{7,8},{8,7},{9,10},{10,... | collective-permute-start | bytes 393224 | tf_op jit(solution)/shard_map/ppermute | solution.py:338
  50.0 1.9 %collective-permute-start.2 = (bf16[512,128]{1,0:T(8,128)(2,1)S(1)}, bf16[512,128]{1,0:T(8,128)(2,1)S(1)}, u32[]{:S(2)}, u32[]{:S(2)}) collective-permute-start(bf16[512,128]{1,0:T(8,128)(2,1)S(1)} %bitcast.25), channel_id=1, source_target_pairs={{0,1},{1,0},{2,3},{3,2},{4,5},{5,4},{6,7},{7,6},{8,9},{9,8},{10,11... | collective-permute-start | bytes 393224 | tf_op jit(solution)/shard_map/ppermute | solution.py:339
  51.9 0.3 observe.1.hot_ref
  52.2 0.2 own.1
  52.4 1.0 %collective-permute-done.3.far_ref = bf16[512,128]{1,0:T(8,128)(2,1)S(1)} collective-permute-done((bf16[512,128]{1,0:T(8,128)(2,1)S(1)}, bf16[512,128]{1,0:T(8,128)(2,1)S(1)}, u32[]{:S(2)}, u32[]{:S(2)}) %collective-permute-start.3) | collective-permute-done | bytes 131104 | tf_op jit(solution)/shard_map/ppermute | solution.py:338
  53.4 0.0 collective-permute-done.2.near_ref
  53.4 2.0 %analysis.1 = bf16[512,128]{1,0:T(8,128)(2,1)S(1)} custom-call(bf16[512,128]{1,0:T(8,128)(2,1)S(1)} %collective-permute-done.2.near_ref, bf16[512,128]{1,0:T(8,128)(2,1)S(1)} %collective-permute-done.3.far_ref, bf16[1536,512]{1,0:T(8,128)(2,1)S(1)} %observe.1.hot_ref, f32[128,512]{1,0:T(8,128)S(1)} %get-tuple-element.34.ens_ref, ...), custom_call_target="tpu_custom_call" | custom-call | tf_op jit(solution)/shard_map/analysis/pallas_call | solution.py:435
  55.4 14.3 %all_to_all.11 = bf16[16,32,128]{2,1,0:T(8,128)(2,1)S(1)} all-to-all(bf16[16,32,128]{2,1,0:T(8,128)(2,1)S(1)} %bitcast.21), channel_id=1, replica_groups=mesh['member'=16,'tile'=64] {'member'}, dimensions={0} | all-to-all | bytes 262144 | tf_op jit(solution)/shard_map/all_to_all | solution.py:444
  69.7 0.8 %unpack.1 = bf16[512,128]{1,0:T(8,128)(2,1)} custom-call(bf16[512,128]{1,0:T(8,128)(2,1)S(1)} %bitcast.23), custom_call_target="tpu_custom_call" | custom-call | tf_op jit(solution)/shard_map/unpack/pallas_call | solution.py:447
Async XLA Ops:
  1.1 21.1 %collective-permute-start = (bf16[96,128]{1,0:T(8,128)(2,1)S(1)}, bf16[96,128]{1,0:T(8,128)(2,1)S(1)}, u32[]{:S(2)}, u32[]{:S(2)}) collective-permute-start(bf16[96,128]{1,0:T(8,128)(2,1)S(1)} %get-tuple-element.24), channel_id=1, source_target_pairs={{0,1},{1,0},{2,3},{3,2},{4,5},{5,4},{6,7},{7,6},{8,9},{9,8},{10,11... | collective-permute-start | bytes 73736 | tf_op jit(solution)/shard_map/ppermute | solution.py:339
  3.0 19.8 %collective-permute-start.1 = (bf16[96,128]{1,0:T(8,128)(2,1)S(1)}, bf16[96,128]{1,0:T(8,128)(2,1)S(1)}, u32[]{:S(2)}, u32[]{:S(2)}) collective-permute-start(bf16[96,128]{1,0:T(8,128)(2,1)S(1)} %get-tuple-element.25), channel_id=1, source_target_pairs={{0,63},{1,2},{2,1},{3,4},{4,3},{5,6},{6,5},{7,8},{8,7},{9,10},{10,... | collective-permute-start | bytes 73736 | tf_op jit(solution)/shard_map/ppermute | solution.py:338
  45.0 8.4 %collective-permute-start.3 = (bf16[512,128]{1,0:T(8,128)(2,1)S(1)}, bf16[512,128]{1,0:T(8,128)(2,1)S(1)}, u32[]{:S(2)}, u32[]{:S(2)}) collective-permute-start(bf16[512,128]{1,0:T(8,128)(2,1)S(1)} %bitcast.24), channel_id=1, source_target_pairs={{0,63},{1,2},{2,1},{3,4},{4,3},{5,6},{6,5},{7,8},{8,7},{9,10},{10,... | collective-permute-start | bytes 393224 | tf_op jit(solution)/shard_map/ppermute | solution.py:338
  50.0 3.4 %collective-permute-start.2 = (bf16[512,128]{1,0:T(8,128)(2,1)S(1)}, bf16[512,128]{1,0:T(8,128)(2,1)S(1)}, u32[]{:S(2)}, u32[]{:S(2)}) collective-permute-start(bf16[512,128]{1,0:T(8,128)(2,1)S(1)} %bitcast.25), channel_id=1, source_target_pairs={{0,1},{1,0},{2,3},{3,2},{4,5},{5,4},{6,7},{7,6},{8,9},{9,8},{10,11... | collective-permute-start | bytes 393224 | tf_op jit(solution)/shard_map/ppermute | solution.py:339

commit v6 on v5

--- a/solution.py
+++ b/solution.py
@@ -51,16 +51,16 @@
     (state_ref, *small), (near_ref, far_ref, wide) = refs[:8], refs[8:11]
     targets, (rows, arrived) = refs[11:18], refs[18:]
     odd = lax.axis_index("tile") % 2
-    loads = cut_copies(state_ref, rows, arrived)
+    load = pltpu.make_async_copy(state_ref, rows, arrived.at[7])
+    load.start()
     others = [
-        pltpu.make_async_copy(source, target, arrived.at[CUTS + number])
+        pltpu.make_async_copy(source, target, arrived.at[number])
         for number, (source, target) in enumerate(zip(small, targets))
     ]
-    for copy in loads + others:
+    for copy in others:
         copy.start()
-    for cut, copy in enumerate(loads):
-        copy.wait()
-        wide[cut * CUT : (cut + 1) * CUT, :] = rows[cut * CUT : (cut + 1) * CUT, :].astype(F32)
+    load.wait()
+    wide[...] = rows[...].astype(F32)
     for row in range(3):
         place = slice(row * 32, (row + 1) * 32)
         near_ref[place, :] = wide[pl.ds(13 * (1 - odd) + row, 32, stride=16), :].astype(BF16)
@@ -134,13 +134,56 @@
     return jnp.dot(weights[...], columns, preferred_element_type=F32)
 
 
-def inner_kernel(wide, weights_ref, inside_ref):
-    for pair in range(4):
-        inside_ref[pair] = silu(first_layer(wide, weights_ref, pair)).astype(BF16)
+def lanes(side):
+    return slice(side * 128, (side + 1) * 128)
+
+
+def joined(taps, side, rows):
+    part = taps[:, lanes(side)].reshape(rows // 16, 3, 16, 128)
+    left, middle, right = (part[:, dx].reshape(rows, 128) for dx in range(3))
+    return middle + pltpu.roll(left, 1, 1) + pltpu.roll(right, 127, 1)
+
+
+def in_turn(tasks, ahead):
+    pending = []
+    for task in tasks:
+        next(task)
+        pending.append(task)
+        if len(pending) > ahead:
+            next(pending.pop(0), None)
+    for task in pending:
+        next(task, None)
+
+
+def inner_kernel(wide, weights_ref, t2_ref, inside_ref, centre_ref):
+    def first(pair):
+        summed = first_layer(wide, weights_ref, pair)
+        yield
+        inside_ref[pair] = silu(summed).astype(BF16)
+
+    def second(pair):
+        taps = jnp.dot(t2_ref[...], inside_ref[pair, 32:288, :], preferred_element_type=F32)
+        yield
+        for side in range(2):
+            centre_ref[pair, :, lanes(side)] = silu(joined(taps, side, 192)).astype(BF16)
+
+    in_turn([first(pair) for pair in range(4)] + [second(pair) for pair in range(4)], 2)
 
 
 def forecast_kernel(
-    wide, near_ref, far_ref, outer_ref, t2_ref, t3_ref, inside, out_ref, edge, outside, h2, sent
+    wide,
+    near_ref,
+    far_ref,
+    outer_ref,
+    t2_ref,
+    t3_ref,
+    inside,
+    centre,
+    out_ref,
+    edge,
+    outside,
+    h2,
+    sent,
 ):
     odd = lax.axis_index("tile") % 2
     for row in range(16):
@@ -155,14 +198,6 @@
         edge[pl.ds(near_at, 32, stride=16), :] = near_ref[place, :].astype(F32)
         edge[pl.ds(far_at, 32, stride=16), :] = far_ref[place, :].astype(F32)
 
-    def lanes(side):
-        return slice(side * 128, (side + 1) * 128)
-
-    def joined(taps, side, rows):
-        part = taps[:, lanes(side)].reshape(rows // 16, 3, 16, 128)
-        left, middle, right = (part[:, dx].reshape(rows, 128) for dx in range(3))
-        return middle + pltpu.roll(left, 1, 1) + pltpu.roll(right, 127, 1)
-
     def first(pair):
         summed = first_layer(edge, outer_ref, pair)
         yield
@@ -171,19 +206,18 @@
     def second(pair, group):
         if group == 0:
             columns = jnp.concatenate([outside[pair, :160, :], inside[pair, :96, :]], axis=0)
-        elif group == 1:
-            columns = inside[pair, 32:288, :]
         else:
             columns = jnp.concatenate([inside[pair, 224:, :], outside[pair, 160:, :]], axis=0)
         taps = jnp.dot(t2_ref[...], columns, preferred_element_type=F32)
         yield
         for side in range(2):
-            h2[pair, group * 192 : (group + 1) * 192, lanes(side)] = silu(
+            h2[pair, group // 2, :, lanes(side)] = silu(
                 joined(taps, side, 192)
             ).astype(BF16)
 
     def third(pair):
-        taps = jnp.dot(t3_ref[...], h2[pair], preferred_element_type=F32)
+        columns = jnp.concatenate([h2[pair, 0], centre[pair], h2[pair, 1]], axis=0)
+        taps = jnp.dot(t3_ref[...], columns, preferred_element_type=F32)
         yield
         for side in range(2):
             member = 2 * pair + side
@@ -191,19 +225,10 @@
             for f in range(4):
                 sent[pl.ds(f * 8 + member, 16, stride=32), :] = result[f * 16 : (f + 1) * 16]
 
-    order = []
-    for pair in range(4):
-        order += [second(pair, 1), first(pair)]
+    order = [first(pair) for pair in range(4)]
     order += [second(pair, group) for group in (0, 2) for pair in range(4)]
     order += [third(pair) for pair in range(4)]
-    pending = []
-    for task in order:
-        next(task)
-        pending.append(task)
-        if len(pending) > 2:
-            next(pending.pop(0), None)
-    for task in pending:
-        next(task, None)
+    in_turn(order, 2)
     out_ref[...] = sent[...].astype(BF16)
 
 
@@ -366,7 +391,7 @@
         + tuple(jax.ShapeDtypeStruct(a.shape, a.dtype) for a in given[1:]),
         in_specs=[HBM] * 8,
         out_specs=(VMEM,) * 10,
-        scratch_shapes=[scratch(512, 128, dtype=BF16), pltpu.SemaphoreType.DMA((CUTS + 7,))],
+        scratch_shapes=[scratch(512, 128, dtype=BF16), pltpu.SemaphoreType.DMA((8,))],
         compiler_params=params(8),
         name="edges",
     )(*(pltpu.with_memory_space_constraint(a, pltpu.HBM) for a in given))
@@ -380,31 +405,34 @@
         cost_estimate=pl.CostEstimate(flops=4000000, bytes_accessed=700000, transcendentals=0),
         name="weights",
     )(first, middle, last)
-    inside = pl.pallas_call(
+    inside, centre = pl.pallas_call(
         inner_kernel,
-        out_shape=jax.ShapeDtypeStruct((4, 320, 256), BF16),
-        in_specs=[VMEM] * 2,
-        out_specs=VMEM,
+        out_shape=(
+            jax.ShapeDtypeStruct((4, 320, 256), BF16),
+            jax.ShapeDtypeStruct((4, 192, 256), BF16),
+        ),
+        in_specs=[VMEM] * 3,
+        out_specs=(VMEM, VMEM),
         compiler_params=params(8),
         cost_estimate=pl.CostEstimate(
-            flops=130000000, bytes_accessed=1000000, transcendentals=330000
+            flops=430000000, bytes_accessed=2000000, transcendentals=530000
         ),
         name="inner",
-    )(wide, inner)
+    )(wide, inner, t2)
     forecast = pl.pallas_call(
         forecast_kernel,
         out_shape=shape(512),
-        in_specs=[VMEM] * 7,
+        in_specs=[VMEM] * 8,
         out_specs=VMEM,
         scratch_shapes=[
             scratch(512, 128),
             scratch(4, 320, 256, dtype=BF16),
-            scratch(4, 576, 256, dtype=BF16),
+            scratch(4, 2, 192, 256, dtype=BF16),
             scratch(512, 128),
         ],
         compiler_params=params(16),
         name="forecast",
-    )(wide, from_near, from_far, outer, t2, t3, inside)
+    )(wide, from_near, from_far, outer, t2, t3, inside, centre)
     own = lax.all_to_all(
         forecast.reshape(16, 32, 128), "member", split_axis=0, concat_axis=0, tiled=True
     ).reshape(512, 128)

time: 70.8 us -> 70.5 us (level)
  transfers between devices with their start and end apart: 4 -> 4, of which waited for: 2 -> 2; matrix products, arithmetic and copies ran while one was open for 0% -> 0% of each run, Pallas kernels for 2% -> 3%
where the time goes in v6:
time: 70.5 us; the launch traced here: 70.2 us
  blocking collectives  34.2 us (49%)
  starting transfers between devices  27.1 us (38%)
  Pallas kernels  7.74 us (11%)
  waiting for transfers between devices  1.06 us (2%)
    ppermute x2, starting transfers between devices, exchange(): from_far = lax.ppermute(far_values, 'tile', far)  23.3 us
    all_to_all x1, blocking collectives, local(): lax.all_to_all(forecast.reshape(16, 32, 128), 'member', split_axis=0, con...  20 us
    all_to_all x1, blocking collectives, local(): lax.all_to_all(analysed.reshape(16, 32, 128), 'member', split_axis=0, con...  14.3 us
    ppermute x2, starting transfers between devices, exchange(): from_near = lax.ppermute(near_values, 'tile', near)  3.84 us
    pallas_call x1, Pallas kernels, local(): pl.pallas_call(analysis_kernel, out_shape=shape(512), in_specs=[VMEM] * 1...  2.01 us
    pallas_call x1, Pallas kernels, local(): pl.pallas_call(forecast_kernel, out_shape=shape(512), in_specs=[VMEM] * 8...  1.98 us
  transfers between devices with their start and end apart: 4, of which 2 were waited for; matrix products, arithmetic and copies ran while one was open for 0% of the time, Pallas kernels for 3%

profile of v6, /device:TPU:2, one launch (start us, length us, event | category | flops | bytes accessed | tf_op | source)
XLA Modules:
  0.0 70.2 jit_solution(15094157300464461832)
XLA Ops:
  0.0 1.0 %edges.1 = (bf16[96,128]{1,0:T(8,128)(2,1)S(1)}, bf16[96,128]{1,0:T(8,128)(2,1)S(1)}, f32[512,128]{1,0:T(8,128)S(1)}, bf16[9,4,32]{2,1,0:T(4,128)(2,1)S(1)}, bf1...) custom-call(bf16[512,128]{1,0:T(8,128)(2,1)} %bitcast.27, ...), custom_call_target="tpu_custom_call" | custom-call | tf_op jit(solution)/shard_map/edges/pallas_call | solution.py:388
  1.1 1.9 %collective-permute-start = (bf16[96,128]{1,0:T(8,128)(2,1)S(1)}, bf16[96,128]{1,0:T(8,128)(2,1)S(1)}, u32[]{:S(2)}, u32[]{:S(2)}) collective-permute-start(bf16[96,128]{1,0:T(8,128)(2,1)S(1)} %get-tuple-element.26), channel_id=1, source_target_pairs={{0,1},{1,0},{2,3},{3,2},{4,5},{5,4},{6,7},{7,6},{8,9},{9,8},{10,11... | collective-permute-start | bytes 73736 | tf_op jit(solution)/shard_map/ppermute | solution.py:364
  3.0 18.3 %collective-permute-start.1 = (bf16[96,128]{1,0:T(8,128)(2,1)S(1)}, bf16[96,128]{1,0:T(8,128)(2,1)S(1)}, u32[]{:S(2)}, u32[]{:S(2)}) collective-permute-start(bf16[96,128]{1,0:T(8,128)(2,1)S(1)} %get-tuple-element.27), channel_id=1, source_target_pairs={{0,63},{1,2},{2,1},{3,4},{4,3},{5,6},{6,5},{7,8},{8,7},{9,10},{10,... | collective-permute-start | bytes 73736 | tf_op jit(solution)/shard_map/ppermute | solution.py:363
  21.3 0.3 weights.1
  21.6 1.0 %inner.1 = (bf16[4,320,256]{2,1,0:T(8,128)(2,1)S(1)}, bf16[4,192,256]{2,1,0:T(8,128)(2,1)S(1)}) custom-call(f32[512,128]{1,0:T(8,128)S(1)} %get-tuple-element.25.wide, bf16[320,192]{1,0:T(8,128)(2,1)S(1)} %get-tuple-element.34.weights_ref, bf16[576,256]{1,0:T(8,128)(2,1)S(1)} %get-tuple-element.32.t2_ref), custom_call_target="tpu_custom_call" | custom-call | flops 430000000 | bytes 2000000 | tf_op jit(solution)/shard_map/inner/pallas_call | solution.py:408
  22.7 0.0 collective-permute-done.near_ref
  22.7 0.1 collective-permute-done.1.far_ref
  22.8 2.0 %forecast.1 = bf16[512,128]{1,0:T(8,128)(2,1)S(1)} custom-call(f32[512,128]{1,0:T(8,128)S(1)} %get-tuple-element.25.wide, bf16[96,128]{1,0:T(8,128)(2,1)S(1)} %collective-permute-done.near_ref, bf16[96,128]{1,0:T(8,128)(2,1)S(1)} %collective-permute-done.1.far_ref, bf16[320,192]{1,0:T(8,128)(2,1)S(1)} %get-tuple-element.31.outer_ref, ...), custom_call_target="tpu_custom_call" | custom-call | tf_op jit(solution)/shard_map/forecast/pallas_call | solution.py:422
  24.8 20.0 %all_to_all.10 = bf16[16,32,128]{2,1,0:T(8,128)(2,1)S(1)} all-to-all(bf16[16,32,128]{2,1,0:T(8,128)(2,1)S(1)} %bitcast.22), channel_id=1, replica_groups=mesh['member'=16,'tile'=64] {'member'}, dimensions={0} | all-to-all | bytes 262144 | tf_op jit(solution)/shard_map/all_to_all | solution.py:436
  44.8 5.0 %collective-permute-start.3 = (bf16[512,128]{1,0:T(8,128)(2,1)S(1)}, bf16[512,128]{1,0:T(8,128)(2,1)S(1)}, u32[]{:S(2)}, u32[]{:S(2)}) collective-permute-start(bf16[512,128]{1,0:T(8,128)(2,1)S(1)} %bitcast.24), channel_id=1, source_target_pairs={{0,63},{1,2},{2,1},{3,4},{4,3},{5,6},{6,5},{7,8},{8,7},{9,10},{10,... | collective-permute-start | bytes 393224 | tf_op jit(solution)/shard_map/ppermute | solution.py:363
  49.7 1.9 %collective-permute-start.2 = (bf16[512,128]{1,0:T(8,128)(2,1)S(1)}, bf16[512,128]{1,0:T(8,128)(2,1)S(1)}, u32[]{:S(2)}, u32[]{:S(2)}) collective-permute-start(bf16[512,128]{1,0:T(8,128)(2,1)S(1)} %bitcast.25), channel_id=1, source_target_pairs={{0,1},{1,0},{2,3},{3,2},{4,5},{5,4},{6,7},{7,6},{8,9},{9,8},{10,11... | collective-permute-start | bytes 393224 | tf_op jit(solution)/shard_map/ppermute | solution.py:364
  51.7 0.3 observe.1.hot_ref
  51.9 0.2 own.1
  52.2 1.0 %collective-permute-done.3.far_ref = bf16[512,128]{1,0:T(8,128)(2,1)S(1)} collective-permute-done((bf16[512,128]{1,0:T(8,128)(2,1)S(1)}, bf16[512,128]{1,0:T(8,128)(2,1)S(1)}, u32[]{:S(2)}, u32[]{:S(2)}) %collective-permute-start.3) | collective-permute-done | bytes 131104 | tf_op jit(solution)/shard_map/ppermute | solution.py:363
  53.1 0.0 collective-permute-done.2.near_ref
  53.1 2.0 %analysis.1 = bf16[512,128]{1,0:T(8,128)(2,1)S(1)} custom-call(bf16[512,128]{1,0:T(8,128)(2,1)S(1)} %collective-permute-done.2.near_ref, bf16[512,128]{1,0:T(8,128)(2,1)S(1)} %collective-permute-done.3.far_ref, bf16[1536,512]{1,0:T(8,128)(2,1)S(1)} %observe.1.hot_ref, f32[128,512]{1,0:T(8,128)S(1)} %get-tuple-element.38.ens_ref, ...), custom_call_target="tpu_custom_call" | custom-call | tf_op jit(solution)/shard_map/analysis/pallas_call | solution.py:463
  55.2 14.3 %all_to_all.11 = bf16[16,32,128]{2,1,0:T(8,128)(2,1)S(1)} all-to-all(bf16[16,32,128]{2,1,0:T(8,128)(2,1)S(1)} %bitcast.21), channel_id=1, replica_groups=mesh['member'=16,'tile'=64] {'member'}, dimensions={0} | all-to-all | bytes 262144 | tf_op jit(solution)/shard_map/all_to_all | solution.py:472
  69.4 0.8 %unpack.1 = bf16[512,128]{1,0:T(8,128)(2,1)} custom-call(bf16[512,128]{1,0:T(8,128)(2,1)S(1)} %bitcast.23), custom_call_target="tpu_custom_call" | custom-call | tf_op jit(solution)/shard_map/unpack/pallas_call | solution.py:475
Async XLA Ops:
  1.1 21.6 %collective-permute-start = (bf16[96,128]{1,0:T(8,128)(2,1)S(1)}, bf16[96,128]{1,0:T(8,128)(2,1)S(1)}, u32[]{:S(2)}, u32[]{:S(2)}) collective-permute-start(bf16[96,128]{1,0:T(8,128)(2,1)S(1)} %get-tuple-element.26), channel_id=1, source_target_pairs={{0,1},{1,0},{2,3},{3,2},{4,5},{5,4},{6,7},{7,6},{8,9},{9,8},{10,11... | collective-permute-start | bytes 73736 | tf_op jit(solution)/shard_map/ppermute | solution.py:364
  3.0 19.8 %collective-permute-start.1 = (bf16[96,128]{1,0:T(8,128)(2,1)S(1)}, bf16[96,128]{1,0:T(8,128)(2,1)S(1)}, u32[]{:S(2)}, u32[]{:S(2)}) collective-permute-start(bf16[96,128]{1,0:T(8,128)(2,1)S(1)} %get-tuple-element.27), channel_id=1, source_target_pairs={{0,63},{1,2},{2,1},{3,4},{4,3},{5,6},{6,5},{7,8},{8,7},{9,10},{10,... | collective-permute-start | bytes 73736 | tf_op jit(solution)/shard_map/ppermute | solution.py:363
  44.8 8.4 %collective-permute-start.3 = (bf16[512,128]{1,0:T(8,128)(2,1)S(1)}, bf16[512,128]{1,0:T(8,128)(2,1)S(1)}, u32[]{:S(2)}, u32[]{:S(2)}) collective-permute-start(bf16[512,128]{1,0:T(8,128)(2,1)S(1)} %bitcast.24), channel_id=1, source_target_pairs={{0,63},{1,2},{2,1},{3,4},{4,3},{5,6},{6,5},{7,8},{8,7},{9,10},{10,... | collective-permute-start | bytes 393224 | tf_op jit(solution)/shard_map/ppermute | solution.py:363
  49.7 3.4 %collective-permute-start.2 = (bf16[512,128]{1,0:T(8,128)(2,1)S(1)}, bf16[512,128]{1,0:T(8,128)(2,1)S(1)}, u32[]{:S(2)}, u32[]{:S(2)}) collective-permute-start(bf16[512,128]{1,0:T(8,128)(2,1)S(1)} %bitcast.25), channel_id=1, source_target_pairs={{0,1},{1,0},{2,3},{3,2},{4,5},{5,4},{6,7},{7,6},{8,9},{9,8},{10,11... | collective-permute-start | bytes 393224 | tf_op jit(solution)/shard_map/ppermute | solution.py:364

commit v7 on v5

--- a/solution.py
+++ b/solution.py
@@ -51,16 +51,16 @@
     (state_ref, *small), (near_ref, far_ref, wide) = refs[:8], refs[8:11]
     targets, (rows, arrived) = refs[11:18], refs[18:]
     odd = lax.axis_index("tile") % 2
-    loads = cut_copies(state_ref, rows, arrived)
+    load = pltpu.make_async_copy(state_ref, rows, arrived.at[7])
+    load.start()
     others = [
-        pltpu.make_async_copy(source, target, arrived.at[CUTS + number])
+        pltpu.make_async_copy(source, target, arrived.at[number])
         for number, (source, target) in enumerate(zip(small, targets))
     ]
-    for copy in loads + others:
+    for copy in others:
         copy.start()
-    for cut, copy in enumerate(loads):
-        copy.wait()
-        wide[cut * CUT : (cut + 1) * CUT, :] = rows[cut * CUT : (cut + 1) * CUT, :].astype(F32)
+    load.wait()
+    wide[...] = rows[...].astype(F32)
     for row in range(3):
         place = slice(row * 32, (row + 1) * 32)
         near_ref[place, :] = wide[pl.ds(13 * (1 - odd) + row, 32, stride=16), :].astype(BF16)
@@ -137,6 +137,11 @@
 def inner_kernel(wide, weights_ref, inside_ref):
     for pair in range(4):
         inside_ref[pair] = silu(first_layer(wide, weights_ref, pair)).astype(BF16)
+
+
+def prepare_kernel(first, middle, last, wide, outer_ref, t2_ref, t3_ref, inside_ref, inner):
+    weights_kernel(first, middle, last, inner, outer_ref, t2_ref, t3_ref)
+    inner_kernel(wide, inner, inside_ref)
 
 
 def forecast_kernel(
@@ -366,31 +371,28 @@
         + tuple(jax.ShapeDtypeStruct(a.shape, a.dtype) for a in given[1:]),
         in_specs=[HBM] * 8,
         out_specs=(VMEM,) * 10,
-        scratch_shapes=[scratch(512, 128, dtype=BF16), pltpu.SemaphoreType.DMA((CUTS + 7,))],
+        scratch_shapes=[scratch(512, 128, dtype=BF16), pltpu.SemaphoreType.DMA((8,))],
         compiler_params=params(8),
         name="edges",
     )(*(pltpu.with_memory_space_constraint(a, pltpu.HBM) for a in given))
     from_near, from_far = exchange(near_edge, far_edge)
-    inner, outer, t2, t3 = pl.pallas_call(
-        weights_kernel,
-        out_shape=(shape(320, 192), shape(320, 192), shape(576, 256), shape(192, 576)),
-        in_specs=[VMEM] * 3,
+    outer, t2, t3, inside = pl.pallas_call(
+        prepare_kernel,
+        out_shape=(
+            shape(320, 192),
+            shape(576, 256),
+            shape(192, 576),
+            jax.ShapeDtypeStruct((4, 320, 256), BF16),
+        ),
+        in_specs=[VMEM] * 4,
         out_specs=(VMEM,) * 4,
-        compiler_params=params(8),
-        cost_estimate=pl.CostEstimate(flops=4000000, bytes_accessed=700000, transcendentals=0),
-        name="weights",
-    )(first, middle, last)
-    inside = pl.pallas_call(
-        inner_kernel,
-        out_shape=jax.ShapeDtypeStruct((4, 320, 256), BF16),
-        in_specs=[VMEM] * 2,
-        out_specs=VMEM,
+        scratch_shapes=[scratch(320, 192, dtype=BF16)],
         compiler_params=params(8),
         cost_estimate=pl.CostEstimate(
-            flops=130000000, bytes_accessed=1000000, transcendentals=330000
+            flops=134000000, bytes_accessed=1700000, transcendentals=330000
         ),
-        name="inner",
-    )(wide, inner)
+        name="prepare",
+    )(first, middle, last, wide)
     forecast = pl.pallas_call(
         forecast_kernel,
         out_shape=shape(512),

time: 70.8 us -> 70.8 us (level)
  no operation moved by 1% of the time
where the time goes in v7:
time: 70.8 us; the launch traced here: 70.5 us
  blocking collectives  34.2 us (48%)
  starting transfers between devices  27.1 us (38%)
  Pallas kernels  7.38 us (10%)
  waiting for transfers between devices  1.64 us (2%)
    ppermute x2, starting transfers between devices, exchange(): from_far = lax.ppermute(far_values, 'tile', far)  23.3 us
    all_to_all x1, blocking collectives, local(): lax.all_to_all(forecast.reshape(16, 32, 128), 'member', split_axis=0, con...  20 us
    all_to_all x1, blocking collectives, local(): lax.all_to_all(analysed.reshape(16, 32, 128), 'member', split_axis=0, con...  14.3 us
    ppermute x2, starting transfers between devices, exchange(): from_near = lax.ppermute(near_values, 'tile', near)  3.84 us
    pallas_call x1, Pallas kernels, local(): pl.pallas_call(forecast_kernel, out_shape=shape(512), in_specs=[VMEM] * 7...  2.2 us
    pallas_call x1, Pallas kernels, local(): pl.pallas_call(analysis_kernel, out_shape=shape(512), in_specs=[VMEM] * 1...  2 us
    ppermute x2, waiting for transfers between devices, exchange(): from_far = lax.ppermute(far_values, 'tile', far)  1.64 us
  transfers between devices with their start and end apart: 4, of which 2 were waited for; matrix products, arithmetic and copies ran while one was open for 0% of the time, Pallas kernels for 2%

profile of v7, /device:TPU:2, one launch (start us, length us, event | category | flops | bytes accessed | tf_op | source)
XLA Modules:
  0.0 70.5 jit_solution(8618992529984958280)
XLA Ops:
  0.0 1.0 %edges.1 = (bf16[96,128]{1,0:T(8,128)(2,1)S(1)}, bf16[96,128]{1,0:T(8,128)(2,1)S(1)}, f32[512,128]{1,0:T(8,128)S(1)}, bf16[9,4,32]{2,1,0:T(4,128)(2,1)S(1)}, bf1...) custom-call(bf16[512,128]{1,0:T(8,128)(2,1)} %bitcast.27, ...), custom_call_target="tpu_custom_call" | custom-call | tf_op jit(solution)/shard_map/edges/pallas_call | solution.py:368
  1.1 1.9 %collective-permute-start = (bf16[96,128]{1,0:T(8,128)(2,1)S(1)}, bf16[96,128]{1,0:T(8,128)(2,1)S(1)}, u32[]{:S(2)}, u32[]{:S(2)}) collective-permute-start(bf16[96,128]{1,0:T(8,128)(2,1)S(1)} %get-tuple-element.24), channel_id=1, source_target_pairs={{0,1},{1,0},{2,3},{3,2},{4,5},{5,4},{6,7},{7,6},{8,9},{9,8},{10,11... | collective-permute-start | bytes 73736 | tf_op jit(solution)/shard_map/ppermute | solution.py:344
  3.0 18.3 %collective-permute-start.1 = (bf16[96,128]{1,0:T(8,128)(2,1)S(1)}, bf16[96,128]{1,0:T(8,128)(2,1)S(1)}, u32[]{:S(2)}, u32[]{:S(2)}) collective-permute-start(bf16[96,128]{1,0:T(8,128)(2,1)S(1)} %get-tuple-element.25), channel_id=1, source_target_pairs={{0,63},{1,2},{2,1},{3,4},{4,3},{5,6},{6,5},{7,8},{8,7},{9,10},{10,... | collective-permute-start | bytes 73736 | tf_op jit(solution)/shard_map/ppermute | solution.py:343
  21.3 0.8 %prepare.1 = (bf16[320,192]{1,0:T(8,128)(2,1)S(1)}, bf16[576,256]{1,0:T(8,128)(2,1)S(1)}, bf16[192,576]{1,0:T(8,128)(2,1)S(1)}, bf16[4,320,256]{2,1,0:T(8,128)(2,1)S(1)}) custom-call(bf16[9,4,32]{2,1,0:T(4,128)(2,1)S(1)} %get-tuple-element.26.first, bf16[9,32,32]{2,1,0:T(8,128)(2,1)S(1)} %get-tuple-element.27.middle, ...), custom_call_target="tpu_custom_call" | custom-call | flops 134000000 | bytes 1700000 | tf_op jit(solution)/shard_map/prepare/pallas_call | solution.py:379
  22.1 0.0 collective-permute-done.near_ref
  22.1 0.7 collective-permute-done.1.far_ref
  22.8 2.2 %forecast.1 = bf16[512,128]{1,0:T(8,128)(2,1)S(1)} custom-call(f32[512,128]{1,0:T(8,128)S(1)} %get-tuple-element.23.wide, bf16[96,128]{1,0:T(8,128)(2,1)S(1)} %collective-permute-done.near_ref, bf16[96,128]{1,0:T(8,128)(2,1)S(1)} %collective-permute-done.1.far_ref, bf16[320,192]{1,0:T(8,128)(2,1)S(1)} %get-tuple-element.29.outer_ref, ...), custom_call_target="tpu_custom_call" | custom-call | tf_op jit(solution)/shard_map/forecast/pallas_call | solution.py:396
  25.0 20.0 %all_to_all.10 = bf16[16,32,128]{2,1,0:T(8,128)(2,1)S(1)} all-to-all(bf16[16,32,128]{2,1,0:T(8,128)(2,1)S(1)} %bitcast.22), channel_id=1, replica_groups=mesh['member'=16,'tile'=64] {'member'}, dimensions={0} | all-to-all | bytes 262144 | tf_op jit(solution)/shard_map/all_to_all | solution.py:410
  45.0 5.0 %collective-permute-start.3 = (bf16[512,128]{1,0:T(8,128)(2,1)S(1)}, bf16[512,128]{1,0:T(8,128)(2,1)S(1)}, u32[]{:S(2)}, u32[]{:S(2)}) collective-permute-start(bf16[512,128]{1,0:T(8,128)(2,1)S(1)} %bitcast.24), channel_id=1, source_target_pairs={{0,63},{1,2},{2,1},{3,4},{4,3},{5,6},{6,5},{7,8},{8,7},{9,10},{10,... | collective-permute-start | bytes 393224 | tf_op jit(solution)/shard_map/ppermute | solution.py:343
  49.9 1.9 %collective-permute-start.2 = (bf16[512,128]{1,0:T(8,128)(2,1)S(1)}, bf16[512,128]{1,0:T(8,128)(2,1)S(1)}, u32[]{:S(2)}, u32[]{:S(2)}) collective-permute-start(bf16[512,128]{1,0:T(8,128)(2,1)S(1)} %bitcast.25), channel_id=1, source_target_pairs={{0,1},{1,0},{2,3},{3,2},{4,5},{5,4},{6,7},{7,6},{8,9},{9,8},{10,11... | collective-permute-start | bytes 393224 | tf_op jit(solution)/shard_map/ppermute | solution.py:344
  51.9 0.3 observe.1.hot_ref
  52.1 0.2 own.1
  52.4 1.0 %collective-permute-done.3.far_ref = bf16[512,128]{1,0:T(8,128)(2,1)S(1)} collective-permute-done((bf16[512,128]{1,0:T(8,128)(2,1)S(1)}, bf16[512,128]{1,0:T(8,128)(2,1)S(1)}, u32[]{:S(2)}, u32[]{:S(2)}) %collective-permute-start.3) | collective-permute-done | bytes 131104 | tf_op jit(solution)/shard_map/ppermute | solution.py:343
  53.4 0.0 collective-permute-done.2.near_ref
  53.4 2.0 %analysis.1 = bf16[512,128]{1,0:T(8,128)(2,1)S(1)} custom-call(bf16[512,128]{1,0:T(8,128)(2,1)S(1)} %collective-permute-done.2.near_ref, bf16[512,128]{1,0:T(8,128)(2,1)S(1)} %collective-permute-done.3.far_ref, bf16[1536,512]{1,0:T(8,128)(2,1)S(1)} %observe.1.hot_ref, f32[128,512]{1,0:T(8,128)S(1)} %get-tuple-element.34.ens_ref, ...), custom_call_target="tpu_custom_call" | custom-call | tf_op jit(solution)/shard_map/analysis/pallas_call | solution.py:437
  55.4 14.3 %all_to_all.11 = bf16[16,32,128]{2,1,0:T(8,128)(2,1)S(1)} all-to-all(bf16[16,32,128]{2,1,0:T(8,128)(2,1)S(1)} %bitcast.21), channel_id=1, replica_groups=mesh['member'=16,'tile'=64] {'member'}, dimensions={0} | all-to-all | bytes 262144 | tf_op jit(solution)/shard_map/all_to_all | solution.py:446
  69.6 0.8 %unpack.1 = bf16[512,128]{1,0:T(8,128)(2,1)} custom-call(bf16[512,128]{1,0:T(8,128)(2,1)S(1)} %bitcast.23), custom_call_target="tpu_custom_call" | custom-call | tf_op jit(solution)/shard_map/unpack/pallas_call | solution.py:449
Async XLA Ops:
  1.1 21.0 %collective-permute-start = (bf16[96,128]{1,0:T(8,128)(2,1)S(1)}, bf16[96,128]{1,0:T(8,128)(2,1)S(1)}, u32[]{:S(2)}, u32[]{:S(2)}) collective-permute-start(bf16[96,128]{1,0:T(8,128)(2,1)S(1)} %get-tuple-element.24), channel_id=1, source_target_pairs={{0,1},{1,0},{2,3},{3,2},{4,5},{5,4},{6,7},{7,6},{8,9},{9,8},{10,11... | collective-permute-start | bytes 73736 | tf_op jit(solution)/shard_map/ppermute | solution.py:344
  3.0 19.8 %collective-permute-start.1 = (bf16[96,128]{1,0:T(8,128)(2,1)S(1)}, bf16[96,128]{1,0:T(8,128)(2,1)S(1)}, u32[]{:S(2)}, u32[]{:S(2)}) collective-permute-start(bf16[96,128]{1,0:T(8,128)(2,1)S(1)} %get-tuple-element.25), channel_id=1, source_target_pairs={{0,63},{1,2},{2,1},{3,4},{4,3},{5,6},{6,5},{7,8},{8,7},{9,10},{10,... | collective-permute-start | bytes 73736 | tf_op jit(solution)/shard_map/ppermute | solution.py:343
  45.0 8.4 %collective-permute-start.3 = (bf16[512,128]{1,0:T(8,128)(2,1)S(1)}, bf16[512,128]{1,0:T(8,128)(2,1)S(1)}, u32[]{:S(2)}, u32[]{:S(2)}) collective-permute-start(bf16[512,128]{1,0:T(8,128)(2,1)S(1)} %bitcast.24), channel_id=1, source_target_pairs={{0,63},{1,2},{2,1},{3,4},{4,3},{5,6},{6,5},{7,8},{8,7},{9,10},{10,... | collective-permute-start | bytes 393224 | tf_op jit(solution)/shard_map/ppermute | solution.py:343
  49.9 3.4 %collective-permute-start.2 = (bf16[512,128]{1,0:T(8,128)(2,1)S(1)}, bf16[512,128]{1,0:T(8,128)(2,1)S(1)}, u32[]{:S(2)}, u32[]{:S(2)}) collective-permute-start(bf16[512,128]{1,0:T(8,128)(2,1)S(1)} %bitcast.25), channel_id=1, source_target_pairs={{0,1},{1,0},{2,3},{3,2},{4,5},{5,4},{6,7},{7,6},{8,9},{9,8},{10,11... | collective-permute-start | bytes 393224 | tf_op jit(solution)/shard_map/ppermute | solution.py:344
